TPU v7x, 32 devices: a whole 2x2x4 slice. The times are simulated.
32 devices in a mesh: segment: 4 (over x, core), rows: 8 (over z, y).
Axes of the slice: x: 2, y: 2, z: 4, core: 2. Of those that a mesh axis runs over, the one named last changes fastest.
Arguments:
- features: bfloat16 [2, 4, 8, 16, 384], P(None, None, 'rows'), may hold values from -6 to 6
- cache_zero: bfloat16 [2, 2, 8, 16, 384], P(None, None, 'rows'), may hold values from -6 to 6
- cache_one: bfloat16 [2, 2, 16, 32, 384], P(None, None, 'rows'), may hold values from -6 to 6
- cache_two: bfloat16 [2, 2, 32, 64, 384], P(None, None, 'rows'), may hold values from -6 to 6
- cache_three: bfloat16 [2, 2, 64, 128, 192], P(None, None, 'rows'), may hold values from -6 to 6
- gain_zero: float32 [384], replicated, may hold values from 0.4 to 1.6
- gain_one: float32 [384], replicated, may hold values from 0.4 to 1.6
- gain_two: float32 [384], replicated, may hold values from 0.4 to 1.6
- gain_three: float32 [192], replicated, may hold values from 0.4 to 1.6
- weight_zero: bfloat16 [1152, 3, 3, 384], P('rows'), may hold values from -0.0625 to 0.0625
- weight_one: bfloat16 [1152, 3, 3, 384], P('rows'), may hold values from -0.0625 to 0.0625
- weight_two: bfloat16 [1152, 3, 3, 192], P('rows'), may hold values from -0.0625 to 0.0625
- weight_three: bfloat16 [576, 3, 3, 96], P('rows'), may hold values from -0.078125 to 0.078125
- proj_two: bfloat16 [384, 192], replicated, may hold values from -0.3125 to 0.3125
- proj_three: bfloat16 [192, 96], replicated, may hold values from -0.4375 to 0.4375
Outputs:
- decoded: bfloat16 [2, 4, 96, 64, 128], P(None, 'segment', None, 'rows')
All inputs are finite; a program needn't handle non-finite values.
Results may differ from a plain program's by a relative error of at most 0.0065.
Values may be sent and summed in bfloat16 or wider, within the bound.
A program may use at most 128 MiB of HBM per device.

v0:
```python
import jax
import jax.numpy as jnp
from jax import lax
from jax.sharding import PartitionSpec as P

EPSILON = 1e-06
BF = jnp.bfloat16
F32 = jnp.float32


def activate(values, gain_vec):
    widened = values.astype(F32)
    scaled = widened * lax.rsqrt(jnp.mean(widened * widened, axis=-1, keepdims=True) + EPSILON)
    return jax.nn.silu(scaled * gain_vec).astype(BF)


def enlarge(values, dim):
    return jnp.repeat(jnp.repeat(values, 2, axis=dim), 2, axis=dim + 1)


def neighbours(array, by):
    size = lax.axis_size("rows")
    up = [(i, i + by) for i in range(size - by)]
    down = [(j, i) for i, j in up]
    return up, down


def from_before(array, by=1):
    size = lax.axis_size("rows")
    return lax.ppermute(array, "rows", [(i, i + by) for i in range(size - by)])


def from_after(array, by=1):
    size = lax.axis_size("rows")
    return lax.ppermute(array, "rows", [(i + by, i) for i in range(size - by)])


def stack_columns(window):
    columns = window.shape[3]
    wide = jnp.pad(window, ((0, 0), (0, 0), (0, 0), (1, 1), (0, 0)))
    return jnp.concatenate(
        [wide[:, :, :, j : j + columns] for j in range(3)], axis=-1
    )


def convolve(window, weight, out_width):
    videos, frames, rows, columns, channels = window.shape
    stacked = stack_columns(window).reshape(-1, 3 * channels)
    product = jnp.dot(stacked, weight, preferred_element_type=F32)
    product = product.reshape(videos, frames, rows, columns, 9 * out_width)
    total = None
    for t in range(3):
        for i in range(3):
            tap = 3 * t + i
            term = product[
                :, t : t + frames - 2, i : i + rows - 2, :, tap * out_width : (tap + 1) * out_width
            ]
            total = term if total is None else total + term
    return total


def shards(
    features,
    cache_zero,
    cache_one,
    cache_two,
    cache_three,
    gain_zero,
    gain_one,
    gain_two,
    gain_three,
    weight_zero,
    weight_one,
    weight_two,
    weight_three,
    proj_two,
    proj_three,
):
    segments = lax.axis_size("segment")
    segment = lax.axis_index("segment")
    row_devices = lax.axis_size("rows")
    row = lax.axis_index("rows")
    frames = features.shape[1]

    def own_channels(array):
        width = array.shape[-1] // segments
        return lax.dynamic_slice_in_dim(array, segment * width, width, array.ndim - 1)

    def gathered(weight):
        return lax.all_gather(
            weight.reshape(weight.shape[0], -1), "rows", axis=0, tiled=True
        )

    full = [
        gathered(own_channels(weight_zero)),
        gathered(own_channels(weight_one)),
        gathered(own_channels(weight_two)),
        gathered(weight_three),
    ]

    def with_rows(array, width):
        rows = array.shape[2]
        before = []
        after = []
        by = 1
        while width > 0:
            take = min(width, rows)
            before.insert(0, from_before(array[:, :, rows - take :], by))
            after.append(from_after(array[:, :, :take], by))
            width -= take
            by += 1
        return jnp.concatenate(before + [array] + after, axis=2)

    def inside(array, halo):
        rows = array.shape[2]
        at = lax.broadcasted_iota(jnp.int32, (1, 1, rows, 1, 1), 2)
        keep = ((at >= halo) | (row > 0)) & ((at < rows - halo) | (row < row_devices - 1))
        return jnp.where(keep, array, jnp.zeros((), array.dtype))

    wide = with_rows(features, 2)
    caches = [
        with_rows(cache_zero, 2),
        with_rows(cache_one, 2),
        with_rows(cache_two, 2),
        with_rows(cache_three, 1),
    ]

    width = weight_zero.shape[3] // segments
    window = jnp.concatenate([caches[0], activate(wide, gain_zero)], axis=1)
    total = convolve(window, full[0], width)
    total = total + own_channels(wide[:, :, 1:-1]).astype(F32)
    mine = inside(total.astype(BF), 1)
    coarse = lax.all_gather(mine, "segment", axis=4, tiled=True)

    width = weight_one.shape[3] // segments
    window = jnp.concatenate([caches[1], enlarge(activate(coarse, gain_one), 2)], axis=1)
    total = convolve(window, full[1], width)
    total = total + enlarge(mine, 2)[:, :, 1:-1].astype(F32)
    mine = inside(total.astype(BF), 1)
    coarse = lax.all_gather(mine, "segment", axis=4, tiled=True)

    width = weight_two.shape[3] // segments
    window = jnp.concatenate([caches[2], enlarge(activate(coarse, gain_two), 2)], axis=1)
    total = convolve(window, full[2], width)
    straight = jnp.dot(
        coarse.reshape(-1, coarse.shape[-1]), own_channels(proj_two), preferred_element_type=F32
    ).reshape(coarse.shape[:-1] + (width,))
    total = total + enlarge(straight, 2)[:, :, 1:-1]
    mine = inside(total.astype(BF), 1)
    coarse = lax.all_gather(mine, "segment", axis=4, tiled=True)

    own = frames // segments
    ahead = jnp.zeros((coarse.shape[0], 2) + coarse.shape[2:], BF)
    recent = lax.dynamic_slice_in_dim(
        jnp.concatenate([ahead, coarse], axis=1), segment * own, own + 2, 1
    )
    newest = enlarge(activate(recent, gain_three), 2)[:, :, 1:-1]
    behind = jnp.pad(caches[3], ((0, 0), (0, frames), (0, 0), (0, 0), (0, 0)))
    behind = lax.dynamic_slice_in_dim(behind, segment * own, own + 2, 1)
    at = segment * own + lax.broadcasted_iota(jnp.int32, (1, own + 2, 1, 1, 1), 1)
    window = jnp.where(at < 2, behind, newest)
    stacked = stack_columns(window)
    videos, _, rows, columns, channels = stacked.shape
    rows -= 2
    out_width = weight_three.shape[3]
    total = None
    for t in range(3):
        for i in range(3):
            tap = 3 * t + i
            block = stacked[:, t : t + own, i : i + rows].reshape(-1, channels)
            term = lax.dot_general(
                full[3][:, tap * out_width : (tap + 1) * out_width],
                block,
                (((0,), (1,)), ((), ())),
                preferred_element_type=F32,
            )
            total = term if total is None else total + term
    mine = recent[:, 2:, 1:-1]
    straight = lax.dot_general(
        proj_three,
        mine.reshape(-1, mine.shape[-1]),
        (((0,), (1,)), ((), ())),
        preferred_element_type=F32,
    ).reshape((out_width,) + mine.shape[:-1])
    total = total.reshape(out_width, videos, own, rows, columns) + enlarge(straight, 3)
    return total.astype(BF).transpose(1, 2, 0, 3, 4)


def solution(mesh):
    slab = P(None, None, "rows", None, None)
    weight = P("rows", None, None, None)
    placed = (slab,) * 5 + (P(),) * 4 + (weight,) * 4 + (P(),) * 2
    return jax.shard_map(
        shards,
        mesh=mesh,
        in_specs=placed,
        out_specs=P(None, "segment", None, "rows", None),
        check_vma=False,
    )
```

profile of v0, /device:TPU:0, one launch (start us, length us, event | category | flops | bytes accessed | tf_op | source)
XLA Modules:
  0.0 469.5 jit_solution(17547927379688148954)
XLA Ops:
  20.2 6.1 %collective-permute-start.6 = (bf16[2,2,1,16,384]{4,3,2,1,0:T(8,128)(2,1)S(1)}, bf16[2,2,1,16,384]{4,3,2,1,0:T(8,128)(2,1)S(1)}, u32[]{:S(2)}, u32[]{:S(2)}) collective-permute-start(bf16[2,2,1,16,384]{4,3,2,1,0:T(8,128)(2,1)S(1)} %copy-done.21), channel_id=1, source_target_pairs={{0,2},{1,3},{2,4},{3,5},{4,6},{5,7},{8,10},{9,11},{10,12},{11,13},... | collective-permute-start | bytes 147464 | tf_op jit(solution)/shard_map/ppermute | solution.py:30
  30.4 38.2 %all_gather.25 = bf16[1152,432]{1,0:T(8,128)(2,1)} all-gather(bf16[144,432]{1,0:T(8,128)(2,1)S(1)} %copy.111), channel_id=1, replica_groups=mesh['segment'=4,'rows'=8] {'rows'}, dimensions={0}, use_global_device_ids=true | all-gather | bytes 1119744 | tf_op jit(solution)/shard_map/all_gather | solution.py:90
  74.0 5.0 %collective-permute-done.8 = bf16[2,2,1,16,384]{4,3,2,1,0:T(8,128)(2,1)S(1)} collective-permute-done((bf16[2,2,1,16,384]{4,3,2,1,0:T(8,128)(2,1)S(1)}, bf16[2,2,1,16,384]{4,3,2,1,0:T(8,128)(2,1)S(1)}, u32[]{:S(2)}, u32[]{:S(2)}) %collective-permute-start.8) | collective-permute-done | bytes 49184 | tf_op jit(solution)/shard_map/ppermute | solution.py:35
  80.3 6.6 %collective-permute-done.9 = bf16[2,2,1,16,384]{4,3,2,1,0:T(8,128)(2,1)S(1)} collective-permute-done((bf16[2,2,1,16,384]{4,3,2,1,0:T(8,128)(2,1)S(1)}, bf16[2,2,1,16,384]{4,3,2,1,0:T(8,128)(2,1)S(1)}, u32[]{:S(2)}, u32[]{:S(2)}) %collective-permute-start.9) | collective-permute-done | bytes 49184 | tf_op jit(solution)/shard_map/ppermute | solution.py:35
  92.2 5.3 %collective-permute-start.2 = (bf16[2,2,2,64,384]{4,3,2,1,0:T(8,128)(2,1)}, bf16[2,2,2,64,384]{4,3,2,1,0:T(8,128)(2,1)}, u32[]{:S(2)}, u32[]{:S(2)}) collective-permute-start(bf16[2,2,2,64,384]{4,3,2,1,0:T(8,128)(2,1)} %get-tuple-element.24), channel_id=1, source_target_pairs={{0,1},{1,2},{2,3},{3,4},{4,5},{5,6},{6,7},{8,9},{9,10},{10,11},{11... | collective-permute-start | bytes 1179656 | tf_op jit(solution)/shard_map/ppermute | solution.py:30
  105.5 17.3 %all_gather.22 = bf16[2,4,3,16,384]{3,1,2,0,4:T(4,128)(2,1)S(1)} all-gather(bf16[2,4,3,16,96]{3,1,2,0,4:T(4,128)(2,1)S(1)} %copy.105), channel_id=1, replica_groups=mesh['segment'=4,'rows'=8] {'segment'}, dimensions={4}, use_global_device_ids=true | all-gather | bytes 368640 | tf_op jit(solution)/shard_map/all_gather | solution.py:133
  134.8 8.6 %fusion.16 = f32[2,6,6,32,864]{4,3,2,1,0:T(8,128)S(1)} fusion(bf16[2,6,6,32,384]{4,3,2,1,0:T(8,128)(2,1)} %get-tuple-element.19, bf16[2,4,6,32,384]{4,3,2,1,0:T(8,128)(2,1)S(1)} %reshape.218, bf16[2,2,2,32,384]{4,3,2,1,0:T(8,128)(2,1)} %collective-permute-done.5, bf16[2,2,2,32,384]{4,3,2,1,0:T(8,128)(2,1)S(1)} %copy-done.18, ...), kind=kOutput, calls=%fused_computation.28 | convolution fusion | flops 4618321920 | bytes 15261696 | tf_op jit(solution)/shard_map/dot_general | solution.py:49
  145.4 22.2 %all_gather.24 = bf16[2,4,4,32,384]{3,2,1,0,4:T(4,128)(2,1)} all-gather(bf16[2,4,4,32,96]{3,2,1,0,4:T(4,128)(2,1)S(1)} %copy.108), channel_id=1, replica_groups=mesh['segment'=4,'rows'=8] {'segment'}, dimensions={4}, use_global_device_ids=true | all-gather | bytes 983040 | tf_op jit(solution)/shard_map/all_gather | solution.py:140
  178.4 7.7 %reshape.223 = bf16[2,4,8,64,384]{4,3,2,1,0:T(8,128)(2,1)} reshape(bf16[2,4,8,32,2,384]{5,4,3,2,1,0:T(2,128)(2,1)} %broadcast_in_dim.104) | data formatting | bytes 6291456 | tf_op jit(solution)/shard_map/reshape | solution.py:18
  190.3 6.6 %fusion.111 = (bf16[2,6,8,64,384]{4,3,2,1,0:T(8,128)(2,1)}, bf16[2,6,8,64,384]{4,3,2,1,0:T(8,128)(2,1)}) fusion(bf16[2,6,8,66,384]{4,3,2,1,0:T(8,128)(2,1)S(1)} %select_maximum_fusion), kind=kLoop, calls=%fused_computation.201 | loop fusion | bytes 18874368 | tf_op jit(solution)/shard_map/slice | solution.py:42
  198.0 23.8 %fusion = f32[2,6,8,64,432]{4,3,2,1,0:T(8,128)S(1)} fusion(bf16[2,6,8,64,384]{4,3,2,1,0:T(8,128)(2,1)} %get-tuple-element.15, bf16[2,4,8,64,384]{4,3,2,1,0:T(8,128)(2,1)} %reshape.223, bf16[2,2,2,64,384]{4,3,2,1,0:T(8,128)(2,1)} %collective-permute-done.3, bf16[2,2,4,64,384]{4,3,2,1,0:T(8,128)(2,1)S(1)} %copy-done.15, ...), kind=kOutput, calls=%fused_computation.2 | convolution fusion | flops 6200229888 | bytes 25767936 | tf_op jit(solution)/shard_map/dot_general | solution.py:49
  237.2 42.6 %all_gather.27 = bf16[576,864]{1,0:T(8,128)(2,1)} all-gather(bf16[72,864]{1,0:T(8,128)(2,1)S(1)} %reshape.230), channel_id=1, replica_groups=mesh['segment'=4,'rows'=8] {'rows'}, dimensions={0}, use_global_device_ids=true | all-gather | bytes 1119744 | tf_op jit(solution)/shard_map/all_gather | solution.py:90
  290.5 9.9 %broadcast_select_fusion = bf16[2,3,10,128,192]{4,0,3,2,1:T(2,128)(2,1)S(1)} fusion(pred[3]{0:T(512)(128)(4,1)S(1)} %add_compare_fusion.1, bf16[2,3,12,128,192]{4,0,3,2,1:T(2,128)(2,1)S(1)} %bitcast.91, s32[]{:T(128)S(6)} %select_n.29, bf16[2,2,1,128,192]{4,0,3,2,1:T(2,128)(2,1)S(1)} %collective-permute-done.1, ...), kind=kLoop, calls=%fused_computation.20 | loop fusion | flops 17694720 | bytes 7865347 | tf_op jit(solution)/shard_map/jit(_where)/select_n | solution.py:161
  300.5 9.8 %pad_slice_fusion.1 = (bf16[2,3,10,128,192]{4,0,3,2,1:T(2,128)(2,1)S(1)}, bf16[2,3,10,128,192]{4,0,3,2,1:T(2,128)(2,1)S(1)}) fusion(bf16[2,3,10,128,192]{4,0,3,2,1:T(2,128)(2,1)S(1)} %broadcast_select_fusion), kind=kLoop, calls=%fused_computation.83 | loop fusion | bytes 8847360 | tf_op jit(solution)/shard_map/slice | solution.py:42
  310.3 18.2 %pad_maximum_fusion = bf16[2,3,10,128,576]{4,0,3,2,1:T(2,128)(2,1)S(1)} fusion(bf16[2,3,10,128,192]{4,0,3,2,1:T(2,128)(2,1)S(1)} %get-tuple-element.17, bf16[2,3,10,128,192]{4,0,3,2,1:T(2,128)(2,1)S(1)} %broadcast_select_fusion, bf16[2,3,10,128,192]{4,0,3,2,1:T(2,128)(2,1)S(1)} %get-tuple-element.16), kind=kLoop, calls=%fused_computation.15 | loop fusion | flops 26542080 | bytes 17694720 | tf_op jit(solution)/shard_map/concatenate | solution.py:41
  328.5 18.6 %fusion.110 = (bf16[2,1,8,128,576]{4,0,3,2,1:T(2,128)(2,1)}, bf16[2,1,8,128,576]{4,0,3,2,1:T(2,128)(2,1)}, bf16[2,1,8,128,576]{4,0,3,2,1:T(2,128)(2,1)}, bf16[2,...) fusion(bf16[2,3,10,128,576]{4,0,3,2,1:T(2,128)(2,1)S(1)} %pad_m, ...), kind=kLoop, calls=%fused_computation.200 | loop fusion | bytes 42467328 | tf_op jit(solution)/shard_map/slice | solution.py:170
  347.1 5.7 %copy.116 = bf16[2,1,8,128,576]{3,2,0,4,1:T(8,128)(2,1)} copy(bf16[2,1,8,128,576]{4,0,3,2,1:T(2,128)(2,1)} %get-tuple-element.13) | data formatting | bytes 4718592 | tf_op jit(solution)/shard_map/slice | solution.py:170
  352.8 4.9 %reshape.229 = bf16[2048,576]{0,1:T(8,128)(2,1)} reshape(bf16[2,1,8,128,576]{3,2,0,4,1:T(8,128)(2,1)} %copy.116) | data formatting | bytes 4718592 | tf_op jit(solution)/shard_map/reshape | solution.py:170
  357.8 5.7 %copy.118 = bf16[2,1,8,128,576]{3,2,0,4,1:T(8,128)(2,1)} copy(bf16[2,1,8,128,576]{4,0,3,2,1:T(2,128)(2,1)} %get-tuple-element.12) | data formatting | bytes 4718592 | tf_op jit(solution)/shard_map/slice | solution.py:170
  368.5 5.7 %copy.119 = bf16[2,1,8,128,576]{3,2,0,4,1:T(8,128)(2,1)} copy(bf16[2,1,8,128,576]{4,0,3,2,1:T(2,128)(2,1)} %get-tuple-element.11) | data formatting | bytes 4718592 | tf_op jit(solution)/shard_map/slice | solution.py:170
  374.2 4.9 %reshape.232 = bf16[2048,576]{0,1:T(8,128)(2,1)} reshape(bf16[2,1,8,128,576]{3,2,0,4,1:T(8,128)(2,1)} %copy.119) | data formatting | bytes 4718592 | tf_op jit(solution)/shard_map/reshape | solution.py:170
  379.1 5.9 %copy.120 = bf16[2,1,8,128,576]{3,2,0,4,1:T(8,128)(2,1)} copy(bf16[2,1,8,128,576]{4,0,3,2,1:T(2,128)(2,1)} %get-tuple-element.10) | data formatting | bytes 4718592 | tf_op jit(solution)/shard_map/slice | solution.py:170
  390.0 5.7 %copy.121 = bf16[2,1,8,128,576]{3,2,0,4,1:T(8,128)(2,1)} copy(bf16[2,1,8,128,576]{4,0,3,2,1:T(2,128)(2,1)} %get-tuple-element.9) | data formatting | bytes 4718592 | tf_op jit(solution)/shard_map/slice | solution.py:170
  395.8 4.9 %reshape.234 = bf16[2048,576]{0,1:T(8,128)(2,1)} reshape(bf16[2,1,8,128,576]{3,2,0,4,1:T(8,128)(2,1)} %copy.121) | data formatting | bytes 4718592 | tf_op jit(solution)/shard_map/reshape | solution.py:170
  400.7 5.7 %copy.122 = bf16[2,1,8,128,576]{3,2,0,4,1:T(8,128)(2,1)} copy(bf16[2,1,8,128,576]{4,0,3,2,1:T(2,128)(2,1)} %get-tuple-element.8) | data formatting | bytes 4718592 | tf_op jit(solution)/shard_map/slice | solution.py:170
  406.4 4.9 %reshape.235 = bf16[2048,576]{0,1:T(8,128)(2,1)} reshape(bf16[2,1,8,128,576]{3,2,0,4,1:T(8,128)(2,1)} %copy.122) | data formatting | bytes 4718592 | tf_op jit(solution)/shard_map/reshape | solution.py:170
  411.4 5.7 %copy.123 = bf16[2,1,8,128,576]{3,2,0,4,1:T(8,128)(2,1)} copy(bf16[2,1,8,128,576]{4,0,3,2,1:T(2,128)(2,1)} %get-tuple-element.7) | data formatting | bytes 4718592 | tf_op jit(solution)/shard_map/slice | solution.py:170
  417.1 4.9 %reshape.236 = bf16[2048,576]{0,1:T(8,128)(2,1)} reshape(bf16[2,1,8,128,576]{3,2,0,4,1:T(8,128)(2,1)} %copy.123) | data formatting | bytes 4718592 | tf_op jit(solution)/shard_map/reshape | solution.py:170
  422.1 5.7 %copy.124 = bf16[2,1,8,128,576]{3,2,0,4,1:T(8,128)(2,1)} copy(bf16[2,1,8,128,576]{4,0,3,2,1:T(2,128)(2,1)} %get-tuple-element.6) | data formatting | bytes 4718592 | tf_op jit(solution)/shard_map/slice | solution.py:170
  427.8 4.9 %reshape.237 = bf16[2048,576]{0,1:T(8,128)(2,1)} reshape(bf16[2,1,8,128,576]{3,2,0,4,1:T(8,128)(2,1)} %copy.124) | data formatting | bytes 4718592 | tf_op jit(solution)/shard_map/reshape | solution.py:170
  432.8 5.7 %copy.125 = bf16[2,1,8,128,576]{3,2,0,4,1:T(8,128)(2,1)} copy(bf16[2,1,8,128,576]{4,0,3,2,1:T(2,128)(2,1)} %get-tuple-element.5) | data formatting | bytes 4718592 | tf_op jit(solution)/shard_map/slice | solution.py:170
  438.5 4.9 %reshape.238 = bf16[2048,576]{0,1:T(8,128)(2,1)} reshape(bf16[2,1,8,128,576]{3,2,0,4,1:T(8,128)(2,1)} %copy.125) | data formatting | bytes 4718592 | tf_op jit(solution)/shard_map/reshape | solution.py:170
  (176 shorter events, 122.0 us)
Async XLA Ops:
  6.5 2.6 copy-start.17
  6.5 13.7 %copy-start.21 = (bf16[2,2,1,16,384]{4,3,2,1,0:T(8,128)(2,1)S(1)}, bf16[2,2,1,16,384]{4,3,2,1,0:T(8,128)(2,1)}, u32[]{:S(2)}) copy-start(bf16[2,2,1,16,384]{4,3,2,1,0:T(8,128)(2,1)} %param.16) | copy-start | bytes 147460
  6.5 93.9 %all-gather.4.cloned.1.call-start = ((), (), s32[]{:S(2)}) async-start(), calls=%async_computation | async-start | bytes 2322432 | tf_op jit(solution)/shard_map/all_gather | solution.py:90
  7.7 21.1 %copy-start.14 = (bf16[2,2,4,64,384]{4,3,2,1,0:T(8,128)(2,1)S(1)}, bf16[2,2,4,64,384]{4,3,2,1,0:T(8,128)(2,1)}, u32[]{:S(2)}) copy-start(bf16[2,2,4,64,384]{4,3,2,1,0:T(8,128)(2,1)} %param.18) | copy-start | bytes 2359300
  8.1 21.8 %copy-start.19 = (bf16[144,3,3,192]{3,0,2,1:T(8,128)(2,1)S(1)}, bf16[144,3,3,192]{3,0,2,1:T(8,128)(2,1)}, u32[]{:S(2)}) copy-start(bf16[144,3,3,192]{3,0,2,1:T(8,128)(2,1)} %param.26) | copy-start | bytes 1492996
  9.1 125.7 %all-gather.6.cloned.1.call-start = ((), (), s32[]{:S(2)}) async-start(), calls=%async_computation.1 | async-start | bytes 2322432 | tf_op jit(solution)/shard_map/all_gather | solution.py:90
  9.2 83.0 %collective-permute-start.11 = (bf16[2,4,1,16,384]{4,3,2,1,0:T(8,128)(2,1)S(1)}, bf16[2,4,1,16,384]{4,3,2,1,0:T(8,128)(2,1)S(1)}, u32[]{:S(2)}, u32[]{:S(2)}) collective-permute-start(bf16[2,4,1,16,384]{4,3,2,1,0:T(8,128)(2,1)S(1)} %copy-done.17), channel_id=1, source_target_pairs={{0,1},{1,2},{2,3},{3,4},{4,5},{5,6},{6,7},{8,9},{9,10},{10,11},{11... | collective-permute-start | bytes 294920 | tf_op jit(solution)/shard_map/ppermute | solution.py:30
  14.1 76.8 %collective-permute-start.10 = (bf16[2,4,1,16,384]{4,3,2,1,0:T(8,128)(2,1)S(1)}, bf16[2,4,1,16,384]{4,3,2,1,0:T(8,128)(2,1)S(1)}, u32[]{:S(2)}, u32[]{:S(2)}) collective-permute-start(bf16[2,4,1,16,384]{4,3,2,1,0:T(8,128)(2,1)S(1)} %copy-done.17), channel_id=1, source_target_pairs={{0,2},{1,3},{2,4},{3,5},{4,6},{5,7},{8,10},{9,11},{10,12},{11,13},... | collective-permute-start | bytes 294920 | tf_op jit(solution)/shard_map/ppermute | solution.py:30
  17.6 80.0 %collective-permute-start.12 = (bf16[2,4,1,16,384]{4,3,2,1,0:T(8,128)(2,1)S(1)}, bf16[2,4,1,16,384]{4,3,2,1,0:T(8,128)(2,1)S(1)}, u32[]{:S(2)}, u32[]{:S(2)}) collective-permute-start(bf16[2,4,1,16,384]{4,3,2,1,0:T(8,128)(2,1)S(1)} %copy-done.17), channel_id=1, source_target_pairs={{1,0},{2,1},{3,2},{4,3},{5,4},{6,5},{7,6},{9,8},{10,9},{11,10},{12... | collective-permute-start | bytes 294920 | tf_op jit(solution)/shard_map/ppermute | solution.py:35
  18.9 80.0 %collective-permute-start.13 = (bf16[2,4,1,16,384]{4,3,2,1,0:T(8,128)(2,1)S(1)}, bf16[2,4,1,16,384]{4,3,2,1,0:T(8,128)(2,1)S(1)}, u32[]{:S(2)}, u32[]{:S(2)}) collective-permute-start(bf16[2,4,1,16,384]{4,3,2,1,0:T(8,128)(2,1)S(1)} %copy-done.17), channel_id=1, source_target_pairs={{2,0},{3,1},{4,2},{5,3},{6,4},{7,5},{10,8},{11,9},{12,10},{13,11},... | collective-permute-start | bytes 294920 | tf_op jit(solution)/shard_map/ppermute | solution.py:35
  20.2 48.5 %collective-permute-start.6 = (bf16[2,2,1,16,384]{4,3,2,1,0:T(8,128)(2,1)S(1)}, bf16[2,2,1,16,384]{4,3,2,1,0:T(8,128)(2,1)S(1)}, u32[]{:S(2)}, u32[]{:S(2)}) collective-permute-start(bf16[2,2,1,16,384]{4,3,2,1,0:T(8,128)(2,1)S(1)} %copy-done.21), channel_id=1, source_target_pairs={{0,2},{1,3},{2,4},{3,5},{4,6},{5,7},{8,10},{9,11},{10,12},{11,13},... | collective-permute-start | bytes 147464 | tf_op jit(solution)/shard_map/ppermute | solution.py:30
  28.8 251.0 %all-gather.8.cloned.1.call-start = ((), (), s32[]{:S(2)}) async-start(), calls=%async_computation.2 | async-start | bytes 2949120 | tf_op jit(solution)/shard_map/all_gather | solution.py:150
  28.9 57.9 %copy-start.18 = (bf16[2,2,2,32,384]{4,3,2,1,0:T(8,128)(2,1)S(1)}, bf16[2,2,2,32,384]{4,3,2,1,0:T(8,128)(2,1)}, u32[]{:S(2)}) copy-start(bf16[2,2,2,32,384]{4,3,2,1,0:T(8,128)(2,1)} %param.17) | copy-start | bytes 589828
  29.9 69.3 %copy-start.23 = (f32[384]{0:T(512)S(1)}, f32[384]{0:T(512)}, u32[]{:S(2)}) copy-start(f32[384]{0:T(512)} %param.20) | copy-start | bytes 4612
  68.7 4.0 collective-permute-start.7
  72.6 6.3 %collective-permute-start.8 = (bf16[2,2,1,16,384]{4,3,2,1,0:T(8,128)(2,1)S(1)}, bf16[2,2,1,16,384]{4,3,2,1,0:T(8,128)(2,1)S(1)}, u32[]{:S(2)}, u32[]{:S(2)}) collective-permute-start(bf16[2,2,1,16,384]{4,3,2,1,0:T(8,128)(2,1)S(1)} %copy-done.21), channel_id=1, source_target_pairs={{1,0},{2,1},{3,2},{4,3},{5,4},{6,5},{7,6},{9,8},{10,9},{11,10},{12... | collective-permute-start | bytes 147464 | tf_op jit(solution)/shard_map/ppermute | solution.py:35
  78.9 7.9 %collective-permute-start.9 = (bf16[2,2,1,16,384]{4,3,2,1,0:T(8,128)(2,1)S(1)}, bf16[2,2,1,16,384]{4,3,2,1,0:T(8,128)(2,1)S(1)}, u32[]{:S(2)}, u32[]{:S(2)}) collective-permute-start(bf16[2,2,1,16,384]{4,3,2,1,0:T(8,128)(2,1)S(1)} %copy-done.21), channel_id=1, source_target_pairs={{2,0},{3,1},{4,2},{5,3},{6,4},{7,5},{10,8},{11,9},{12,10},{13,11},... | collective-permute-start | bytes 147464 | tf_op jit(solution)/shard_map/ppermute | solution.py:35
  86.8 39.7 %collective-permute-start.4 = (bf16[2,2,2,32,384]{4,3,2,1,0:T(8,128)(2,1)S(1)}, bf16[2,2,2,32,384]{4,3,2,1,0:T(8,128)(2,1)}, u32[]{:S(2)}, u32[]{:S(2)}) collective-permute-start(bf16[2,2,2,32,384]{4,3,2,1,0:T(8,128)(2,1)S(1)} %copy-done.18), channel_id=1, source_target_pairs={{0,1},{1,2},{2,3},{3,4},{4,5},{5,6},{6,7},{8,9},{9,10},{10,11},{11... | collective-permute-start | bytes 589832 | tf_op jit(solution)/shard_map/ppermute | solution.py:30
  90.9 35.6 %collective-permute-start.5 = (bf16[2,2,2,32,384]{4,3,2,1,0:T(8,128)(2,1)S(1)}, bf16[2,2,2,32,384]{4,3,2,1,0:T(8,128)(2,1)}, u32[]{:S(2)}, u32[]{:S(2)}) collective-permute-start(bf16[2,2,2,32,384]{4,3,2,1,0:T(8,128)(2,1)S(1)} %copy-done.18), channel_id=1, source_target_pairs={{1,0},{2,1},{3,2},{4,3},{5,4},{6,5},{7,6},{9,8},{10,9},{11,10},{12... | collective-permute-start | bytes 589832 | tf_op jit(solution)/shard_map/ppermute | solution.py:35
  92.2 93.8 %collective-permute-start.2 = (bf16[2,2,2,64,384]{4,3,2,1,0:T(8,128)(2,1)}, bf16[2,2,2,64,384]{4,3,2,1,0:T(8,128)(2,1)}, u32[]{:S(2)}, u32[]{:S(2)}) collective-permute-start(bf16[2,2,2,64,384]{4,3,2,1,0:T(8,128)(2,1)} %get-tuple-element.24), channel_id=1, source_target_pairs={{0,1},{1,2},{2,3},{3,4},{4,5},{5,6},{6,7},{8,9},{9,10},{10,11},{11... | collective-permute-start | bytes 1179656 | tf_op jit(solution)/shard_map/ppermute | solution.py:30
  97.6 88.4 %collective-permute-start.3 = (bf16[2,2,2,64,384]{4,3,2,1,0:T(8,128)(2,1)}, bf16[2,2,2,64,384]{4,3,2,1,0:T(8,128)(2,1)}, u32[]{:S(2)}, u32[]{:S(2)}) collective-permute-start(bf16[2,2,2,64,384]{4,3,2,1,0:T(8,128)(2,1)} %get-tuple-element.25), channel_id=1, source_target_pairs={{1,0},{2,1},{3,2},{4,3},{5,4},{6,5},{7,6},{9,8},{10,9},{11,10},{12... | collective-permute-start | bytes 1179656 | tf_op jit(solution)/shard_map/ppermute | solution.py:35
  105.4 19.5 %copy-start.24 = (f32[384]{0:T(512)S(1)}, f32[384]{0:T(512)}, u32[]{:S(2)}) copy-start(f32[384]{0:T(512)} %param.21) | copy-start | bytes 4612
  167.6 5.2 %copy-start.25 = (f32[384]{0:T(512)S(1)}, f32[384]{0:T(512)}, u32[]{:S(2)}) copy-start(f32[384]{0:T(512)} %param.22) | copy-start | bytes 4612
  178.4 7.7 %copy-start.15 = (bf16[2,2,4,64,384]{4,3,2,1,0:T(8,128)(2,1)S(1)}, bf16[2,2,4,64,384]{4,3,2,1,0:T(8,128)(2,1)}, u32[]{:S(2)}) copy-start(bf16[2,2,4,64,384]{4,3,2,1,0:T(8,128)(2,1)} %param.18) | copy-start | bytes 2359300
  190.3 7.8 %copy-start.16 = (bf16[1152,432]{1,0:T(8,128)(2,1)S(1)}, bf16[1152,432]{1,0:T(8,128)(2,1)}, u32[]{:S(2)}) copy-start(bf16[1152,432]{1,0:T(8,128)(2,1)} %all_gather.25) | copy-start | bytes 2985988
  226.9 10.0 %copy-start.20 = (bf16[72,3,3,96]{3,0,2,1:T(8,128)(2,1)S(1)}, bf16[72,3,3,96]{3,0,2,1:T(8,128)(2,1)}, u32[]{:S(2)}) copy-start(bf16[72,3,3,96]{3,0,2,1:T(8,128)(2,1)} %param.27) | copy-start | bytes 373252
  231.8 48.0 %copy-start.10 = (bf16[2,2,8,128,192]{4,0,3,2,1:T(2,128)(2,1)}, bf16[2,2,8,128,192]{4,0,3,2,1:T(2,128)(2,1)S(1)}, u32[]{:S(2)}) copy-start(bf16[2,2,8,128,192]{4,0,3,2,1:T(2,128)(2,1)S(1)} %copy.101) | copy-start | bytes 4718596
  233.2 52.5 %collective-permute-start = (bf16[2,2,1,128,192]{4,0,3,2,1:T(2,128)(2,1)}, bf16[2,2,1,128,192]{4,0,3,2,1:T(2,128)(2,1)S(1)}, u32[]{:S(2)}, u32[]{:S(2)}) collective-permute-start(bf16[2,2,1,128,192]{4,0,3,2,1:T(2,128)(2,1)} %get-tuple-element.20), channel_id=1, source_target_pairs={{0,1},{1,2},{2,3},{3,4},{4,5},{5,6},{6,7},{8,9},{9,10},{10,11},{11... | collective-permute-start | bytes 589832 | tf_op jit(solution)/shard_map/ppermute | solution.py:30
  235.6 50.0 %collective-permute-start.1 = (bf16[2,2,1,128,192]{4,0,3,2,1:T(2,128)(2,1)S(1)}, bf16[2,2,1,128,192]{4,0,3,2,1:T(2,128)(2,1)S(1)}, u32[]{:S(2)}, u32[]{:S(2)}) collective-permute-start(bf16[2,2,1,128,192]{4,0,3,2,1:T(2,128)(2,1)S(1)} %get-tuple-element.21), channel_id=1, source_target_pairs={{1,0},{2,1},{3,2},{4,3},{5,4},{6,5},{7,6},{9,8},{10,9},{11,10},{12... | collective-permute-start | bytes 589832 | tf_op jit(solution)/shard_map/ppermute | solution.py:35
  279.8 3.8 copy-start.26
  287.9 2.6 copy-start.11
  443.5 2.7 copy-start.12
  (12 other events, 20.0 us)
Sparse Core Ops, SparseCore 0:
  9.5 67.8 all-gather.3
  79.6 55.1 all-gather.5
  227.1 22.1 all-gather.7
where the time goes:
time: 478 us; the launch traced here: 469 us
  local copies, waits for them, and re-layouts  192 us (40%)
  blocking collectives  120 us (25%)
  matrix products  45.8 us (10%)
  other arithmetic  42.2 us (9%)
  starting transfers between devices  37.7 us (8%)
  waiting for transfers between devices  16.8 us (4%)
  between operations  14.4 us (3%)
    all_gather x2, blocking collectives, gathered(): lax.all_gather(weight.reshape(weight.shape[0], -1), 'rows', axis=0, tiled...  80.8 us
    slice x10, local copies, waits for them, and re-layouts, shards(): block = stacked[:, t:t + own, i:i + rows].reshape(-1, channels)  70.5 us
    reshape x9, local copies, waits for them, and re-layouts, shards(): block = stacked[:, t:t + own, i:i + rows].reshape(-1, channels)  44.5 us
    all_gather x2, blocking collectives, shards(): coarse = lax.all_gather(mine, 'segment', axis=4, tiled=True)  39.5 us
    dot_general x3, matrix products, convolve(): product = jnp.dot(stacked, weight, preferred_element_type=F32)  36.7 us
    ppermute x7, starting transfers between devices, from_before(): return lax.ppermute(array, 'rows', [(i, i + by) for i in range(size - by)])  28.6 us
    slice x4, local copies, waits for them, and re-layouts, stack_columns(): wide[:, :, :, j:j + columns]  19.6 us
    concatenate x1, other arithmetic, stack_columns(): jnp.concatenate([wide[:, :, :, j:j + columns] for j in range(3)], axis=-1)  18.2 us
  transfers between devices with their start and end apart: 17, of which 4 were waited for; matrix products, arithmetic and copies ran while one was open for 13% of the time, Pallas kernels for 0%

commit v1 on v0

--- a/solution.py
+++ b/solution.py
@@ -1,6 +1,8 @@
 import jax
 import jax.numpy as jnp
 from jax import lax
+from jax.experimental import pallas as pl
+from jax.experimental.pallas import tpu as pltpu
 from jax.sharding import PartitionSpec as P
 
 EPSILON = 1e-06
@@ -16,13 +18,6 @@
 
 def enlarge(values, dim):
     return jnp.repeat(jnp.repeat(values, 2, axis=dim), 2, axis=dim + 1)
-
-
-def neighbours(array, by):
-    size = lax.axis_size("rows")
-    up = [(i, i + by) for i in range(size - by)]
-    down = [(j, i) for i, j in up]
-    return up, down
 
 
 def from_before(array, by=1):
@@ -57,6 +52,212 @@
             ]
             total = term if total is None else total + term
     return total
+
+
+def selector(rows, columns, offset, fine, transposed=False):
+    shape = (columns, rows) if transposed else (rows, columns)
+    source = lax.broadcasted_iota(jnp.int32, shape, 1 if transposed else 0) + offset
+    at = lax.broadcasted_iota(jnp.int32, shape, 0 if transposed else 1)
+    hit = (source == at) if fine else ((source == 2 * at) | (source == 2 * at + 1))
+    return jnp.where(hit, 1.0, 0.0).astype(BF)
+
+
+def picked(a, b):
+    return jnp.dot(a, b, preferred_element_type=F32).astype(BF)
+
+
+def middle_kernel(cache_ref, low_ref, straight_ref, weight_ref, proj_ref, keep_ref, out_ref, stacked, product, plain):
+    _, past, rows, columns, channels = cache_ref.shape
+    frames = low_ref.shape[1]
+    width = proj_ref.shape[1]
+    half = columns // 2
+    line = rows * columns
+    inner = rows - 2
+    for j in range(3):
+        fine = selector(columns, columns, j - 1, True)
+        coarse = selector(columns, half, j - 1, False)
+        lanes = slice(j * channels, (j + 1) * channels)
+
+        def old(w, _):
+            for q in range(rows):
+                at = pl.multiple_of(w * line + q * columns, columns)
+                stacked[pl.ds(at, columns), lanes] = picked(fine, cache_ref[0, w, q])
+            return 0
+
+        def new(f, _):
+            for l in range(rows // 2):
+                row = picked(coarse, low_ref[0, f, l])
+                at = pl.multiple_of((f + past) * line + 2 * l * columns, columns)
+                stacked[pl.ds(at, columns), lanes] = row
+                stacked[pl.ds(at + columns, columns), lanes] = row
+            return 0
+
+        lax.fori_loop(0, past, old, 0)
+        lax.fori_loop(0, frames, new, 0)
+
+    coarse = selector(columns, half, 0, False)
+
+    def multiply(w, _):
+        at = pl.multiple_of(w * line, line)
+        product[w] = jnp.dot(
+            stacked[pl.ds(at, line), :], weight_ref[...], preferred_element_type=F32
+        )
+        return 0
+
+    lax.fori_loop(0, frames + past, multiply, 0)
+
+    for f in range(frames):
+        for q in range(inner):
+            plain[q * columns : (q + 1) * columns, :] = picked(
+                coarse, straight_ref[0, f, (q + 1) // 2]
+            )
+        total = jnp.dot(plain[...], proj_ref[...], preferred_element_type=F32)
+        for t in range(3):
+            for i in range(3):
+                tap = 3 * t + i
+                total = total + product[
+                    f + t,
+                    i * columns : (i + inner) * columns,
+                    tap * width : (tap + 1) * width,
+                ]
+        total = jnp.where(keep_ref[...] > 0.0, total, 0.0)
+        out_ref[0, :, f * inner * columns : (f + 1) * inner * columns] = total.T.astype(BF)
+
+
+def middle(cache, low, straight, weight, proj, keep):
+    videos, past, rows, columns, channels = cache.shape
+    frames = low.shape[1]
+    width = proj.shape[1]
+    cells = (rows - 2) * columns
+
+    def one(shape):
+        return pl.BlockSpec((1,) + shape[1:], lambda v: (v,) + (0,) * (len(shape) - 1))
+
+    def whole(shape):
+        return pl.BlockSpec(shape, lambda v: (0,) * len(shape))
+
+    return pl.pallas_call(
+        middle_kernel,
+        grid=(videos,),
+        in_specs=[
+            one(cache.shape),
+            one(low.shape),
+            one(straight.shape),
+            whole(weight.shape),
+            whole(proj.shape),
+            whole(keep.shape),
+        ],
+        out_specs=one((videos, width, frames * cells)),
+        out_shape=jax.ShapeDtypeStruct((videos, width, frames * cells), BF),
+        scratch_shapes=[
+            pltpu.VMEM(((frames + past) * rows * columns, 3 * channels), BF),
+            pltpu.VMEM((frames + past, rows * columns, weight.shape[1]), F32),
+            pltpu.VMEM((cells, channels), BF),
+        ],
+        compiler_params=pltpu.CompilerParams(vmem_limit_bytes=56 * 1024 * 1024),
+        name="middle",
+    )(cache, low, straight, weight, proj, keep)
+
+
+def last_kernel(old_ref, cache_ref, low_ref, straight_ref, weight_ref, proj_ref, out_ref, stacked, plain, held):
+    videos, taken, rows, channels, columns = cache_ref.shape
+    half = columns // 2
+    inner = rows - 2
+
+    def spread(offset):
+        pair = (2 * half, 2 * columns)
+        source = lax.broadcasted_iota(jnp.int32, pair, 1)
+        second = source >= columns
+        source = jnp.where(second, source - columns, source) + offset
+        at = lax.broadcasted_iota(jnp.int32, pair, 0)
+        lower = at >= half
+        at = jnp.where(lower, at - half, at)
+        hit = ((source == 2 * at) | (source == 2 * at + 1)) & (second == lower)
+        return jnp.where(hit, 1.0, 0.0).astype(BF)
+
+    def put(t, j, q, value):
+        stacked[t, j * channels : (j + 1) * channels, q * columns : (q + 1) * columns] = value
+
+    for t in range(3):
+        flag = old_ref[t]
+
+        @pl.when(flag > 0)
+        def _():
+            for j in range(3):
+                fine = selector(columns, columns, j - 1, True, transposed=True)
+                for q in range(rows):
+                    put(t, j, q, picked(cache_ref[0, t, q], fine))
+
+        @pl.when(flag == 0)
+        def _():
+            for j in range(3):
+                coarse = spread(j - 1)
+                for p in range((rows + 2) // 4):
+                    at = (t * (rows // 2 + 1) + 2 * p) * half
+                    both = picked(low_ref[0, :, at : at + 2 * half], coarse)
+                    for part in range(2):
+                        for q in (4 * p + 2 * part - 1, 4 * p + 2 * part):
+                            if 0 <= q < rows:
+                                put(t, j, q, both[:, part * columns : (part + 1) * columns])
+
+    coarse = spread(0)
+    for p in range((rows + 2) // 4):
+        at = 2 * p * half
+        both = picked(straight_ref[0, :, at : at + 2 * half], coarse)
+        for part in range(2):
+            for q in (4 * p + 2 * part - 1, 4 * p + 2 * part):
+                if 1 <= q <= inner:
+                    plain[:, (q - 1) * columns : q * columns] = both[
+                        :, part * columns : (part + 1) * columns
+                    ]
+
+    total = jnp.dot(proj_ref[...], plain[...], preferred_element_type=F32)
+    for t in range(3):
+        for i in range(3):
+            total = total + jnp.dot(
+                weight_ref[3 * t + i],
+                stacked[t, :, i * columns : (i + inner) * columns],
+                preferred_element_type=F32,
+            )
+    for q in range(inner):
+        held[:, q, :] = total[:, q * columns : (q + 1) * columns]
+    out_ref[0, 0] = held[...].astype(BF)
+
+
+def last(old, cache, low, straight, weight, proj):
+    videos, taken, rows, channels, columns = cache.shape
+    width = proj.shape[0]
+
+    def one(shape):
+        return pl.BlockSpec((1,) + shape[1:], lambda v, old: (v,) + (0,) * (len(shape) - 1))
+
+    def whole(shape):
+        return pl.BlockSpec(shape, lambda v, old: (0,) * len(shape))
+
+    out = (videos, 1, width, rows - 2, columns)
+    return pl.pallas_call(
+        last_kernel,
+        grid_spec=pltpu.PrefetchScalarGridSpec(
+            num_scalar_prefetch=1,
+            grid=(videos,),
+            in_specs=[
+                one(cache.shape),
+                one(low.shape),
+                one(straight.shape),
+                whole(weight.shape),
+                whole(proj.shape),
+            ],
+            out_specs=one(out),
+            scratch_shapes=[
+                pltpu.VMEM((3, 3 * channels, rows * columns), BF),
+                pltpu.VMEM((channels, (rows - 2) * columns), BF),
+                pltpu.VMEM((width, rows - 2, columns), F32),
+            ],
+        ),
+        out_shape=jax.ShapeDtypeStruct(out, BF),
+        compiler_params=pltpu.CompilerParams(vmem_limit_bytes=56 * 1024 * 1024),
+        name="last",
+    )(old, cache, low, straight, weight, proj)
 
 
 def shards(
@@ -140,50 +341,39 @@
     coarse = lax.all_gather(mine, "segment", axis=4, tiled=True)
 
     width = weight_two.shape[3] // segments
-    window = jnp.concatenate([caches[2], enlarge(activate(coarse, gain_two), 2)], axis=1)
-    total = convolve(window, full[2], width)
-    straight = jnp.dot(
-        coarse.reshape(-1, coarse.shape[-1]), own_channels(proj_two), preferred_element_type=F32
-    ).reshape(coarse.shape[:-1] + (width,))
-    total = total + enlarge(straight, 2)[:, :, 1:-1]
-    mine = inside(total.astype(BF), 1)
-    coarse = lax.all_gather(mine, "segment", axis=4, tiled=True)
+    rows = caches[2].shape[2] - 2
+    columns = caches[2].shape[3]
+    at = lax.broadcasted_iota(jnp.int32, (rows * columns, 1), 0) // columns
+    keep = ((at >= 1) | (row > 0)) & ((at < rows - 1) | (row < row_devices - 1))
+    mine = middle(
+        caches[2],
+        activate(coarse, gain_two),
+        coarse,
+        full[2],
+        own_channels(proj_two),
+        keep.astype(F32),
+    )
+    coarse = lax.all_gather(mine, "segment", axis=1, tiled=True)
 
     own = frames // segments
-    ahead = jnp.zeros((coarse.shape[0], 2) + coarse.shape[2:], BF)
+    videos, channels = coarse.shape[:2]
+    cells = rows * columns
+    ahead = jnp.zeros((videos, channels, 2 * cells), BF)
     recent = lax.dynamic_slice_in_dim(
-        jnp.concatenate([ahead, coarse], axis=1), segment * own, own + 2, 1
-    )
-    newest = enlarge(activate(recent, gain_three), 2)[:, :, 1:-1]
-    behind = jnp.pad(caches[3], ((0, 0), (0, frames), (0, 0), (0, 0), (0, 0)))
-    behind = lax.dynamic_slice_in_dim(behind, segment * own, own + 2, 1)
-    at = segment * own + lax.broadcasted_iota(jnp.int32, (1, own + 2, 1, 1, 1), 1)
-    window = jnp.where(at < 2, behind, newest)
-    stacked = stack_columns(window)
-    videos, _, rows, columns, channels = stacked.shape
-    rows -= 2
-    out_width = weight_three.shape[3]
-    total = None
-    for t in range(3):
-        for i in range(3):
-            tap = 3 * t + i
-            block = stacked[:, t : t + own, i : i + rows].reshape(-1, channels)
-            term = lax.dot_general(
-                full[3][:, tap * out_width : (tap + 1) * out_width],
-                block,
-                (((0,), (1,)), ((), ())),
-                preferred_element_type=F32,
-            )
-            total = term if total is None else total + term
-    mine = recent[:, 2:, 1:-1]
-    straight = lax.dot_general(
-        proj_three,
-        mine.reshape(-1, mine.shape[-1]),
-        (((0,), (1,)), ((), ())),
-        preferred_element_type=F32,
-    ).reshape((out_width,) + mine.shape[:-1])
-    total = total.reshape(out_width, videos, own, rows, columns) + enlarge(straight, 3)
-    return total.astype(BF).transpose(1, 2, 0, 3, 4)
+        jnp.concatenate([ahead, coarse], axis=2), segment * own * cells, (own + 2) * cells, 2
+    )
+    widened = recent.astype(F32)
+    widened = widened * lax.rsqrt(
+        jnp.mean(widened * widened, axis=1, keepdims=True) + EPSILON
+    )
+    newest = jax.nn.silu(widened * gain_three[:, None]).astype(BF)
+    behind = caches[3].transpose(0, 1, 2, 4, 3)
+    behind = jnp.pad(behind, ((0, 0), (0, own), (0, 0), (0, 0), (0, 0)))
+    swapped = jnp.concatenate([behind[:, 1:2], behind[:, 2:3], behind[:, 2:3]], axis=1)
+    behind = jnp.where(segment * own == 0, behind, swapped)
+    old = (segment * own + jnp.arange(own + 2, dtype=jnp.int32) < 2).astype(jnp.int32)
+    taps = full[3].reshape(full[3].shape[0], 9, -1).transpose(1, 2, 0)
+    return last(old, behind, newest, recent[:, :, 2 * cells :], taps, proj_three.T)
 
 
 def solution(mesh):

time: 478 us -> 304 us (0.64); the launches traced: 469 us -> 303 us
  local copies, waits for them, and re-layouts: 192 us -> 32.6 us
  Pallas kernels: 0 us -> 36.5 us
  matrix products: 45.8 us -> 13.1 us
  other arithmetic: 42.2 us -> 17.9 us
  waiting for transfers between devices: 16.8 us -> 28.3 us
    slice x11 -> x3, local copies, waits for them, and re-layouts: 70.5 us -> 2.01 us  [the longest x1 1.75 us: shards(): recent[:, :, 2 * cells:]]
    reshape x11 -> x0, local copies, waits for them, and re-layouts: 46.1 us -> none  [the longest x9 44.5 us: shards(): block = stacked[:, t:t + own, i:i + rows].reshape(-1, channels)]
    pallas_call x0 -> x2, Pallas kernels: none -> 36.5 us  [the longest x1 25.4 us: middle(): pl.pallas_call(middle_kernel, grid=(videos,), in_specs=[one(cache.shape),...]
    dot_general x3 -> x2, matrix products: 36.7 us -> 13.1 us  [convolve(): product = jnp.dot(stacked, weight, preferred_element_type=F32)]
    concatenate x2 -> x1, other arithmetic: 22.4 us -> 1.38 us  [with_rows(): return jnp.concatenate(before + [array] + after, axis=2)]
    ppermute x7, waiting for transfers between devices: 1.73 us -> 17.6 us  [from_before(): return lax.ppermute(array, 'rows', [(i, i + by) for i in range(size - by)])]
    slice x4 -> x2, local copies, waits for them, and re-layouts: 19.6 us -> 4.1 us  [stack_columns(): wide[:, :, :, j:j + columns]]
    broadcast_in_dim x12 -> x4, local copies, waits for them, and re-layouts: 12.2 us -> 1.12 us  [enlarge(): return jnp.repeat(jnp.repeat(values, 2, axis=dim), 2, axis=dim + 1)]
where the time goes in v1:
time: 304 us; the launch traced here: 303 us
  blocking collectives  119 us (39%)
  starting transfers between devices  41.1 us (14%)
  Pallas kernels  36.5 us (12%)
  local copies, waits for them, and re-layouts  32.6 us (11%)
  waiting for transfers between devices  28.3 us (9%)
  other arithmetic  17.9 us (6%)
  between operations  13.7 us (5%)
  matrix products  13.1 us (4%)
    all_gather x2, blocking collectives, gathered(): lax.all_gather(weight.reshape(weight.shape[0], -1), 'rows', axis=0, tiled...  80.1 us
    all_gather x2, blocking collectives, shards(): coarse = lax.all_gather(mine, 'segment', axis=4, tiled=True)  39.3 us
    ppermute x7, starting transfers between devices, from_before(): return lax.ppermute(array, 'rows', [(i, i + by) for i in range(size - by)])  31.8 us
    pallas_call x1, Pallas kernels, middle(): pl.pallas_call(middle_kernel, grid=(videos,), in_specs=[one(cache.shape),...  25.4 us
    ppermute x7, waiting for transfers between devices, from_before(): return lax.ppermute(array, 'rows', [(i, i + by) for i in range(size - by)])  17.6 us
    dot_general x2, matrix products, convolve(): product = jnp.dot(stacked, weight, preferred_element_type=F32)  13.1 us
    pallas_call x1, Pallas kernels, last(): pl.pallas_call(last_kernel, grid_spec=pltpu.PrefetchScalarGridSpec(num_sc...  11.1 us
    ppermute x7, waiting for transfers between devices, from_after(): return lax.ppermute(array, 'rows', [(i + by, i) for i in range(size - by)])  10.7 us
  transfers between devices with their start and end apart: 17, of which 4 were waited for; matrix products, arithmetic and copies ran while one was open for 13% of the time, Pallas kernels for 0%

profile of v1, /device:TPU:0, one launch (start us, length us, event | category | flops | bytes accessed | tf_op | source)
XLA Modules:
  0.0 302.6 jit_solution(2395757037395432051)
XLA Ops:
  9.2 4.9 %collective-permute-start.11 = (bf16[2,4,1,16,384]{4,3,2,1,0:T(8,128)(2,1)S(1)}, bf16[2,4,1,16,384]{4,3,2,1,0:T(8,128)(2,1)S(1)}, u32[]{:S(2)}, u32[]{:S(2)}) collective-permute-start(bf16[2,4,1,16,384]{4,3,2,1,0:T(8,128)(2,1)S(1)} %copy-done.4), channel_id=1, source_target_pairs={{0,1},{1,2},{2,3},{3,4},{4,5},{5,6},{6,7},{8,9},{9,10},{10,11},{11... | collective-permute-start | bytes 294920 | tf_op jit(solution)/shard_map/ppermute | solution.py:25
  14.1 4.1 %collective-permute-start.10 = (bf16[2,4,1,16,384]{4,3,2,1,0:T(8,128)(2,1)S(1)}, bf16[2,4,1,16,384]{4,3,2,1,0:T(8,128)(2,1)}, u32[]{:S(2)}, u32[]{:S(2)}) collective-permute-start(bf16[2,4,1,16,384]{4,3,2,1,0:T(8,128)(2,1)S(1)} %copy-done.4), channel_id=1, source_target_pairs={{0,2},{1,3},{2,4},{3,5},{4,6},{5,7},{8,10},{9,11},{10,12},{11,13},... | collective-permute-start | bytes 294920 | tf_op jit(solution)/shard_map/ppermute | solution.py:25
  20.8 6.8 %collective-permute-start.6 = (bf16[2,2,1,16,384]{4,3,2,1,0:T(8,128)(2,1)}, bf16[2,2,1,16,384]{4,3,2,1,0:T(8,128)(2,1)}, u32[]{:S(2)}, u32[]{:S(2)}) collective-permute-start(bf16[2,2,1,16,384]{4,3,2,1,0:T(8,128)(2,1)} %param.16), channel_id=1, source_target_pairs={{0,2},{1,3},{2,4},{3,5},{4,6},{5,7},{8,10},{9,11},{10,12},{11,13},... | collective-permute-start | bytes 147464 | tf_op jit(solution)/shard_map/ppermute | solution.py:25
  31.4 38.2 %all_gather.25.weight_ref = bf16[1152,432]{1,0:T(8,128)(2,1)} all-gather(bf16[144,432]{1,0:T(8,128)(2,1)S(1)} %copy.49), channel_id=1, replica_groups=mesh['segment'=4,'rows'=8] {'rows'}, dimensions={0}, use_global_device_ids=true | all-gather | bytes 1119744 | tf_op jit(solution)/shard_map/all_gather | solution.py:291
  72.5 2.0 collective-permute-start.7
  78.7 4.3 %collective-permute-done.8 = bf16[2,2,1,16,384]{4,3,2,1,0:T(8,128)(2,1)S(1)} collective-permute-done((bf16[2,2,1,16,384]{4,3,2,1,0:T(8,128)(2,1)}, bf16[2,2,1,16,384]{4,3,2,1,0:T(8,128)(2,1)S(1)}, u32[]{:S(2)}, u32[]{:S(2)}) %collective-permute-start.8) | collective-permute-done | bytes 49184 | tf_op jit(solution)/shard_map/ppermute | solution.py:30
  84.3 6.4 %collective-permute-done.9 = bf16[2,2,1,16,384]{4,3,2,1,0:T(8,128)(2,1)S(1)} collective-permute-done((bf16[2,2,1,16,384]{4,3,2,1,0:T(8,128)(2,1)}, bf16[2,2,1,16,384]{4,3,2,1,0:T(8,128)(2,1)S(1)}, u32[]{:S(2)}, u32[]{:S(2)}) %collective-permute-start.9) | collective-permute-done | bytes 49184 | tf_op jit(solution)/shard_map/ppermute | solution.py:30
  90.6 5.0 %collective-permute-start.4 = (bf16[2,2,2,32,384]{4,3,2,1,0:T(8,128)(2,1)}, bf16[2,2,2,32,384]{4,3,2,1,0:T(8,128)(2,1)}, u32[]{:S(2)}, u32[]{:S(2)}) collective-permute-start(bf16[2,2,2,32,384]{4,3,2,1,0:T(8,128)(2,1)} %param.17), channel_id=1, source_target_pairs={{0,1},{1,2},{2,3},{3,4},{4,5},{5,6},{6,7},{8,9},{9,10},{10,11},{11... | collective-permute-start | bytes 589832 | tf_op jit(solution)/shard_map/ppermute | solution.py:25
  95.7 1.3 collective-permute-start.5
  97.9 4.6 %collective-permute-start.2 = (bf16[2,2,2,64,384]{4,3,2,1,0:T(8,128)(2,1)}, bf16[2,2,2,64,384]{4,3,2,1,0:T(8,128)(2,1)S(1)}, u32[]{:S(2)}, u32[]{:S(2)}) collective-permute-start(bf16[2,2,2,64,384]{4,3,2,1,0:T(8,128)(2,1)} %get-tuple-element.11), channel_id=1, source_target_pairs={{0,1},{1,2},{2,3},{3,4},{4,5},{5,6},{6,7},{8,9},{9,10},{10,11},{11... | collective-permute-start | bytes 1179656 | tf_op jit(solution)/shard_map/ppermute | solution.py:25
  107.2 16.3 %collective-permute-done.2 = bf16[2,2,2,64,384]{4,3,2,1,0:T(8,128)(2,1)S(1)} collective-permute-done((bf16[2,2,2,64,384]{4,3,2,1,0:T(8,128)(2,1)}, bf16[2,2,2,64,384]{4,3,2,1,0:T(8,128)(2,1)S(1)}, u32[]{:S(2)}, u32[]{:S(2)}) %collective-permute-start.2) | collective-permute-done | bytes 393248 | tf_op jit(solution)/shard_map/ppermute | solution.py:25
  123.5 1.4 pad_maximum_fusion.cache_ref
  124.9 4.5 %fusion.16 = f32[2,6,5,16,864]{4,3,2,1,0:T(8,128)S(1)} fusion(bf16[2,6,5,16,384]{4,3,2,1,0:T(8,128)(2,1)} %get-tuple-element.10, bf16[2,4,5,16,384]{4,3,2,1,0:T(8,128)(2,1)S(1)} %fusion.53, bf16[2,2,5,16,384]{4,3,2,1,0:T(8,128)(2,1)} %copy-done.9, bf16[2,6,5,16,384]{4,3,2,1,0:T(8,128)(2,1)S(1)} %get-tuple-element.9, ...), kind=kOutput, calls=%fused_computation.23 | convolution fusion | flops 1919877120 | bytes 7520256 | tf_op jit(solution)/shard_map/dot_general | solution.py:44
  131.0 17.3 %all_gather.22 = bf16[2,4,3,16,384]{3,1,2,0,4:T(4,128)(2,1)S(1)} all-gather(bf16[2,4,3,16,96]{3,1,2,0,4:T(4,128)(2,1)} %copy.43), channel_id=1, replica_groups=mesh['segment'=4,'rows'=8] {'segment'}, dimensions={4}, use_global_device_ids=true | all-gather | bytes 368640 | tf_op jit(solution)/shard_map/all_gather | solution.py:334
  148.3 3.2 %copy.44 = bf16[2,4,3,16,384]{4,3,2,1,0:T(8,128)(2,1)} copy(bf16[2,4,3,16,384]{3,1,2,0,4:T(4,128)(2,1)S(1)} %all_gather.22) | data formatting | bytes 589824 | tf_op jit(solution)/shard_map/all_gather | solution.py:334
  155.2 2.1 select_maximum_fusion
  157.3 2.9 fusion.79
  160.1 8.6 %fusion = f32[2,6,6,32,864]{4,3,2,1,0:T(8,128)S(1)} fusion(bf16[2,6,6,32,384]{4,3,2,1,0:T(8,128)(2,1)} %get-tuple-element.6, bf16[2,4,6,32,384]{4,3,2,1,0:T(8,128)(2,1)S(1)} %reshape.185, bf16[2,2,2,32,384]{4,3,2,1,0:T(8,128)(2,1)} %collective-permute-done.5, bf16[2,2,2,32,384]{4,3,2,1,0:T(8,128)(2,1)} %param.17, ...), kind=kOutput, calls=%fused_computation.2 | convolution fusion | flops 4618321920 | bytes 15261696 | tf_op jit(solution)/shard_map/dot_general | solution.py:44
  170.7 22.0 %all_gather.24 = bf16[2,4,4,32,384]{3,2,1,0,4:T(4,128)(2,1)} all-gather(bf16[2,4,4,32,96]{3,2,1,0,4:T(4,128)(2,1)S(1)} %copy.46), channel_id=1, replica_groups=mesh['segment'=4,'rows'=8] {'segment'}, dimensions={4}, use_global_device_ids=true | all-gather | bytes 983040 | tf_op jit(solution)/shard_map/all_gather | solution.py:341
  192.7 4.9 %copy.47.straight_ref = bf16[2,4,4,32,384]{4,3,2,1,0:T(8,128)(2,1)S(1)} copy(bf16[2,4,4,32,384]{3,2,1,0,4:T(4,128)(2,1)} %all_gather.24) | data formatting | bytes 1572864 | tf_op jit(solution)/shard_map/all_gather | solution.py:341
  197.9 1.4 fusion.44.low_ref
  199.3 25.4 %middle.1 = bf16[2,48,1536]{2,1,0:T(8,128)(2,1)} custom-call(bf16[2,2,8,64,384]{4,3,2,1,0:T(8,128)(2,1)} %pad_maximum_fusion.cache_ref, bf16[2,4,4,32,384]{4,3,2,1,0:T(8,128)(2,1)} %fusion.44.low_ref, bf16[2,4,4,32,384]{4,3,2,1,0:T(8,128)(2,1)} %copy-done.1, bf16[1152,432]{1,0:T(8,128)(2,1)} %all_gather.25.weight_ref, bf16[384,48]{1,0:T(8,128)(2,1)} %copy.57.proj_ref, ...), custom_call_target="tpu_custom_call" | custom-call | tf_op jit(solution)/shard_map/middle/pallas_call | solution.py:139
  225.8 4.4 %collective-permute-start = (bf16[2,2,1,128,192]{3,4,2,1,0:T(8,128)(2,1)S(1)}, bf16[2,2,1,128,192]{3,4,2,1,0:T(8,128)(2,1)S(1)}, u32[]{:S(2)}, u32[]{:S(2)}) collective-permute-start(bf16[2,2,1,128,192]{3,4,2,1,0:T(8,128)(2,1)S(1)} %get-tuple-element.7), channel_id=1, source_target_pairs={{0,1},{1,2},{2,3},{3,4},{4,5},{5,6},{6,7},{8,9},{9,10},{10,11},{11... | collective-permute-start | bytes 589832 | tf_op jit(solution)/shard_map/ppermute | solution.py:25
  230.2 1.5 collective-permute-start.1
  232.0 41.9 %all_gather.27 = bf16[576,864]{1,0:T(8,128)(2,1)S(1)} all-gather(bf16[72,864]{1,0:T(8,128)(2,1)S(1)} %reshape.190), channel_id=1, replica_groups=mesh['segment'=4,'rows'=8] {'rows'}, dimensions={0}, use_global_device_ids=true | all-gather | bytes 1119744 | tf_op jit(solution)/shard_map/all_gather | solution.py:291
  273.9 1.4 copy.53
  276.6 1.7 maximum_bitcast_fusion
  278.5 1.8 maximum_select_fusion.cache_ref
  280.3 1.3 fusion.27
  281.6 1.8 pad_dynamic-slice_fusion.straight_ref
  283.4 1.6 fusion.34.low_ref
  285.0 11.1 %last.1 = bf16[2,1,96,8,128]{4,3,2,1,0:T(8,128)(2,1)} custom-call(s32[3]{0:T(128)} %compare_convert_fusion.old_ref, bf16[2,3,10,192,128]{4,3,2,1,0:T(8,128)(2,1)} %maximum_select_fusion.cache_ref, bf16[2,192,1152]{2,1,0:T(8,128)(2,1)} %fusion.34.low_ref, bf16[2,192,384]{2,1,0:T(8,128)(2,1)} %pad_dynamic-slice_fusion.straight_ref, ...), custom_call_target="tpu_custom_call" | custom-call | tf_op jit(solution)/shard_map/last/pallas_call | solution.py:238
  (113 shorter events, 33.1 us)
Async XLA Ops:
  6.5 118.3 %all-gather.4.cloned.1.call-start = ((), (), s32[]{:S(2)}) async-start(), calls=%async_computation | async-start | bytes 2322432 | tf_op jit(solution)/shard_map/all_gather | solution.py:291
  7.9 22.9 %copy-start.10 = (bf16[144,3,3,192]{3,0,2,1:T(8,128)(2,1)S(1)}, bf16[144,3,3,192]{3,0,2,1:T(8,128)(2,1)}, u32[]{:S(2)}) copy-start(bf16[144,3,3,192]{3,0,2,1:T(8,128)(2,1)} %param.26) | copy-start | bytes 1492996
  9.1 151.0 %all-gather.6.cloned.1.call-start = ((), (), s32[]{:S(2)}) async-start(), calls=%async_computation.1 | async-start | bytes 2322432 | tf_op jit(solution)/shard_map/all_gather | solution.py:291
  9.2 88.7 %collective-permute-start.11 = (bf16[2,4,1,16,384]{4,3,2,1,0:T(8,128)(2,1)S(1)}, bf16[2,4,1,16,384]{4,3,2,1,0:T(8,128)(2,1)S(1)}, u32[]{:S(2)}, u32[]{:S(2)}) collective-permute-start(bf16[2,4,1,16,384]{4,3,2,1,0:T(8,128)(2,1)S(1)} %copy-done.4), channel_id=1, source_target_pairs={{0,1},{1,2},{2,3},{3,4},{4,5},{5,6},{6,7},{8,9},{9,10},{10,11},{11... | collective-permute-start | bytes 294920 | tf_op jit(solution)/shard_map/ppermute | solution.py:25
  14.1 81.6 %collective-permute-start.10 = (bf16[2,4,1,16,384]{4,3,2,1,0:T(8,128)(2,1)S(1)}, bf16[2,4,1,16,384]{4,3,2,1,0:T(8,128)(2,1)}, u32[]{:S(2)}, u32[]{:S(2)}) collective-permute-start(bf16[2,4,1,16,384]{4,3,2,1,0:T(8,128)(2,1)S(1)} %copy-done.4), channel_id=1, source_target_pairs={{0,2},{1,3},{2,4},{3,5},{4,6},{5,7},{8,10},{9,11},{10,12},{11,13},... | collective-permute-start | bytes 294920 | tf_op jit(solution)/shard_map/ppermute | solution.py:25
  18.2 84.3 %collective-permute-start.12 = (bf16[2,4,1,16,384]{4,3,2,1,0:T(8,128)(2,1)S(1)}, bf16[2,4,1,16,384]{4,3,2,1,0:T(8,128)(2,1)S(1)}, u32[]{:S(2)}, u32[]{:S(2)}) collective-permute-start(bf16[2,4,1,16,384]{4,3,2,1,0:T(8,128)(2,1)S(1)} %copy-done.4), channel_id=1, source_target_pairs={{1,0},{2,1},{3,2},{4,3},{5,4},{6,5},{7,6},{9,8},{10,9},{11,10},{12... | collective-permute-start | bytes 294920 | tf_op jit(solution)/shard_map/ppermute | solution.py:30
  19.5 84.4 %collective-permute-start.13 = (bf16[2,4,1,16,384]{4,3,2,1,0:T(8,128)(2,1)S(1)}, bf16[2,4,1,16,384]{4,3,2,1,0:T(8,128)(2,1)}, u32[]{:S(2)}, u32[]{:S(2)}) collective-permute-start(bf16[2,4,1,16,384]{4,3,2,1,0:T(8,128)(2,1)S(1)} %copy-done.4), channel_id=1, source_target_pairs={{2,0},{3,1},{4,2},{5,3},{6,4},{7,5},{10,8},{11,9},{12,10},{13,11},... | collective-permute-start | bytes 294920 | tf_op jit(solution)/shard_map/ppermute | solution.py:30
  20.8 51.7 %collective-permute-start.6 = (bf16[2,2,1,16,384]{4,3,2,1,0:T(8,128)(2,1)}, bf16[2,2,1,16,384]{4,3,2,1,0:T(8,128)(2,1)}, u32[]{:S(2)}, u32[]{:S(2)}) collective-permute-start(bf16[2,2,1,16,384]{4,3,2,1,0:T(8,128)(2,1)} %param.16), channel_id=1, source_target_pairs={{0,2},{1,3},{2,4},{3,5},{4,6},{5,7},{8,10},{9,11},{10,12},{11,13},... | collective-permute-start | bytes 147464 | tf_op jit(solution)/shard_map/ppermute | solution.py:25
  29.0 41.4 %copy-start.3 = (bf16[2,2,4,64,384]{4,3,2,1,0:T(8,128)(2,1)S(1)}, bf16[2,2,4,64,384]{4,3,2,1,0:T(8,128)(2,1)}, u32[]{:S(2)}) copy-start(bf16[2,2,4,64,384]{4,3,2,1,0:T(8,128)(2,1)} %param.18) | copy-start | bytes 2359300
  30.1 250.3 %all-gather.8.cloned.1.call-start = ((), (), s32[]{:S(2)}) async-start(), calls=%async_computation.2 | async-start | bytes 1474560 | tf_op jit(solution)/shard_map/all_gather | solution.py:356
  69.6 35.5 %copy-start.13 = (f32[384]{0:T(512)S(1)}, f32[384]{0:T(512)}, u32[]{:S(2)}) copy-start(f32[384]{0:T(512)} %param.20) | copy-start | bytes 4612
  72.5 4.1 %collective-permute-start.7 = (bf16[2,2,1,16,384]{4,3,2,1,0:T(8,128)(2,1)}, bf16[2,2,1,16,384]{4,3,2,1,0:T(8,128)(2,1)S(1)}, u32[]{:S(2)}, u32[]{:S(2)}) collective-permute-start(bf16[2,2,1,16,384]{4,3,2,1,0:T(8,128)(2,1)} %param.16), channel_id=1, source_target_pairs={{0,1},{1,2},{2,3},{3,4},{4,5},{5,6},{6,7},{8,9},{9,10},{10,11},{11... | collective-permute-start | bytes 147464 | tf_op jit(solution)/shard_map/ppermute | solution.py:25
  76.6 6.4 %collective-permute-start.8 = (bf16[2,2,1,16,384]{4,3,2,1,0:T(8,128)(2,1)}, bf16[2,2,1,16,384]{4,3,2,1,0:T(8,128)(2,1)S(1)}, u32[]{:S(2)}, u32[]{:S(2)}) collective-permute-start(bf16[2,2,1,16,384]{4,3,2,1,0:T(8,128)(2,1)} %param.16), channel_id=1, source_target_pairs={{1,0},{2,1},{3,2},{4,3},{5,4},{6,5},{7,6},{9,8},{10,9},{11,10},{12... | collective-permute-start | bytes 147464 | tf_op jit(solution)/shard_map/ppermute | solution.py:30
  83.0 7.7 %collective-permute-start.9 = (bf16[2,2,1,16,384]{4,3,2,1,0:T(8,128)(2,1)}, bf16[2,2,1,16,384]{4,3,2,1,0:T(8,128)(2,1)S(1)}, u32[]{:S(2)}, u32[]{:S(2)}) collective-permute-start(bf16[2,2,1,16,384]{4,3,2,1,0:T(8,128)(2,1)} %param.16), channel_id=1, source_target_pairs={{2,0},{3,1},{4,2},{5,3},{6,4},{7,5},{10,8},{11,9},{12,10},{13,11},... | collective-permute-start | bytes 147464 | tf_op jit(solution)/shard_map/ppermute | solution.py:30
  90.6 64.6 %collective-permute-start.4 = (bf16[2,2,2,32,384]{4,3,2,1,0:T(8,128)(2,1)}, bf16[2,2,2,32,384]{4,3,2,1,0:T(8,128)(2,1)}, u32[]{:S(2)}, u32[]{:S(2)}) collective-permute-start(bf16[2,2,2,32,384]{4,3,2,1,0:T(8,128)(2,1)} %param.17), channel_id=1, source_target_pairs={{0,1},{1,2},{2,3},{3,4},{4,5},{5,6},{6,7},{8,9},{9,10},{10,11},{11... | collective-permute-start | bytes 589832 | tf_op jit(solution)/shard_map/ppermute | solution.py:25
  95.7 9.7 %copy-start.9 = (bf16[2,2,5,16,384]{4,3,2,1,0:T(8,128)(2,1)}, bf16[2,2,5,16,384]{4,3,2,1,0:T(8,128)(2,1)S(1)}, u32[]{:S(2)}) copy-start(bf16[2,2,5,16,384]{4,3,2,1,0:T(8,128)(2,1)S(1)} %constant_dynamic-update-slice_fusion) | copy-start | bytes 737284
  95.7 59.5 %collective-permute-start.5 = (bf16[2,2,2,32,384]{4,3,2,1,0:T(8,128)(2,1)}, bf16[2,2,2,32,384]{4,3,2,1,0:T(8,128)(2,1)}, u32[]{:S(2)}, u32[]{:S(2)}) collective-permute-start(bf16[2,2,2,32,384]{4,3,2,1,0:T(8,128)(2,1)} %param.17), channel_id=1, source_target_pairs={{1,0},{2,1},{3,2},{4,3},{5,4},{6,5},{7,6},{9,8},{10,9},{11,10},{12... | collective-permute-start | bytes 589832 | tf_op jit(solution)/shard_map/ppermute | solution.py:30
  97.9 7.5 %copy-start.5 = (bf16[2,4,1,16,384]{4,3,2,1,0:T(8,128)(2,1)}, bf16[2,4,1,16,384]{4,3,2,1,0:T(8,128)(2,1)S(1)}, u32[]{:S(2)}) copy-start(bf16[2,4,1,16,384]{4,3,2,1,0:T(8,128)(2,1)S(1)} %collective-permute-done.11) | copy-start | bytes 294916
  97.9 25.6 %collective-permute-start.2 = (bf16[2,2,2,64,384]{4,3,2,1,0:T(8,128)(2,1)}, bf16[2,2,2,64,384]{4,3,2,1,0:T(8,128)(2,1)S(1)}, u32[]{:S(2)}, u32[]{:S(2)}) collective-permute-start(bf16[2,2,2,64,384]{4,3,2,1,0:T(8,128)(2,1)} %get-tuple-element.11), channel_id=1, source_target_pairs={{0,1},{1,2},{2,3},{3,4},{4,5},{5,6},{6,7},{8,9},{9,10},{10,11},{11... | collective-permute-start | bytes 1179656 | tf_op jit(solution)/shard_map/ppermute | solution.py:25
  102.6 2.9 copy-start.7
  102.6 20.9 %collective-permute-start.3 = (bf16[2,2,2,64,384]{4,3,2,1,0:T(8,128)(2,1)S(1)}, bf16[2,2,2,64,384]{4,3,2,1,0:T(8,128)(2,1)S(1)}, u32[]{:S(2)}, u32[]{:S(2)}) collective-permute-start(bf16[2,2,2,64,384]{4,3,2,1,0:T(8,128)(2,1)S(1)} %get-tuple-element.12), channel_id=1, source_target_pairs={{1,0},{2,1},{3,2},{4,3},{5,4},{6,5},{7,6},{9,8},{10,9},{11,10},{12... | collective-permute-start | bytes 1179656 | tf_op jit(solution)/shard_map/ppermute | solution.py:30
  124.9 4.6 %copy-start.6 = (bf16[2,4,1,16,384]{4,3,2,1,0:T(8,128)(2,1)S(1)}, bf16[2,4,1,16,384]{4,3,2,1,0:T(8,128)(2,1)}, u32[]{:S(2)}) copy-start(bf16[2,4,1,16,384]{4,3,2,1,0:T(8,128)(2,1)} %copy-done.5) | copy-start | bytes 294916
  124.9 4.6 %copy-start.8 = (bf16[2,4,1,16,384]{4,3,2,1,0:T(8,128)(2,1)S(1)}, bf16[2,4,1,16,384]{4,3,2,1,0:T(8,128)(2,1)}, u32[]{:S(2)}) copy-start(bf16[2,4,1,16,384]{4,3,2,1,0:T(8,128)(2,1)} %copy-done.7) | copy-start | bytes 294916
  148.3 4.3 %copy-start.14 = (f32[384]{0:T(512)S(1)}, f32[384]{0:T(512)}, u32[]{:S(2)}) copy-start(f32[384]{0:T(512)} %param.21) | copy-start | bytes 4612
  160.1 8.9 %copy-start.17 = (pred[4]{0:T(512)(128)(4,1)S(1)}, pred[4]{0:T(512)(128)(4,1)}, u32[]{:S(2)}) copy-start(pred[4]{0:T(512)(128)(4,1)} %or_and_fusion.1) | copy-start | bytes 16
  192.7 5.2 %copy-start.15 = (f32[384]{0:T(512)S(1)}, f32[384]{0:T(512)}, u32[]{:S(2)}) copy-start(f32[384]{0:T(512)} %param.22) | copy-start | bytes 4612
  199.3 32.5 %copy-start.11 = (bf16[72,3,3,96]{3,0,2,1:T(8,128)(2,1)S(1)}, bf16[72,3,3,96]{3,0,2,1:T(8,128)(2,1)}, u32[]{:S(2)}) copy-start(bf16[72,3,3,96]{3,0,2,1:T(8,128)(2,1)} %param.27) | copy-start | bytes 373252
  225.8 49.5 %copy-start.12 = (bf16[192,96]{1,0:T(8,128)(2,1)S(1)}, bf16[192,96]{1,0:T(8,128)(2,1)}, u32[]{:S(2)}) copy-start(bf16[192,96]{1,0:T(8,128)(2,1)} %param.29) | copy-start | bytes 110596
  225.8 50.8 %collective-permute-start = (bf16[2,2,1,128,192]{3,4,2,1,0:T(8,128)(2,1)S(1)}, bf16[2,2,1,128,192]{3,4,2,1,0:T(8,128)(2,1)S(1)}, u32[]{:S(2)}, u32[]{:S(2)}) collective-permute-start(bf16[2,2,1,128,192]{3,4,2,1,0:T(8,128)(2,1)S(1)} %get-tuple-element.7), channel_id=1, source_target_pairs={{0,1},{1,2},{2,3},{3,4},{4,5},{5,6},{6,7},{8,9},{9,10},{10,11},{11... | collective-permute-start | bytes 589832 | tf_op jit(solution)/shard_map/ppermute | solution.py:25
  230.2 46.3 %collective-permute-start.1 = (bf16[2,2,1,128,192]{3,4,2,1,0:T(8,128)(2,1)S(1)}, bf16[2,2,1,128,192]{3,4,2,1,0:T(8,128)(2,1)S(1)}, u32[]{:S(2)}, u32[]{:S(2)}) collective-permute-start(bf16[2,2,1,128,192]{3,4,2,1,0:T(8,128)(2,1)S(1)} %get-tuple-element.8), channel_id=1, source_target_pairs={{1,0},{2,1},{3,2},{4,3},{5,4},{6,5},{7,6},{9,8},{10,9},{11,10},{12... | collective-permute-start | bytes 589832 | tf_op jit(solution)/shard_map/ppermute | solution.py:30
  280.3 3.1 %copy-start.16 = (f32[192]{0:T(256)S(1)}, f32[192]{0:T(256)}, u32[]{:S(2)}) copy-start(f32[192]{0:T(256)} %param.23) | copy-start | bytes 2308
  280.3 3.1 %copy-start.2 = (bf16[2,192,1536]{2,1,0:T(8,128)(2,1)S(1)}, bf16[2,192,1536]{2,1,0:T(8,128)(2,1)}, u32[]{:S(2)}) copy-start(bf16[2,192,1536]{2,1,0:T(8,128)(2,1)} %all-gather.8.cloned.1.call-done) | copy-start | bytes 3538948
  (3 other events, 5.6 us)
Sparse Core Ops, SparseCore 0:
  9.5 67.2 all-gather.3
  79.0 60.2 all-gather.5
  224.9 21.9 all-gather.7

commit v2 on v1

--- a/solution.py
+++ b/solution.py
@@ -1,3 +1,5 @@
+import functools
+
 import jax
 import jax.numpy as jnp
 from jax import lax
@@ -20,14 +22,224 @@
     return jnp.repeat(jnp.repeat(values, 2, axis=dim), 2, axis=dim + 1)
 
 
-def from_before(array, by=1):
+MESH = pl.DeviceIdType.MESH
+
+
+def ring_place(row, size):
+    return jnp.where(row % 2 == 0, row // 2, size - 1 - row // 2)
+
+
+def ring_row(place, size):
+    return jnp.where(place < size // 2, 2 * place, 2 * (size - 1 - place) + 1)
+
+
+def halo_plan(shapes, widths):
+    plan = []
+    for k, (shape, width) in enumerate(zip(shapes, widths)):
+        by = 1
+        while width > 0:
+            take = min(width, shape[2])
+            plan.append((k, by, take))
+            width -= take
+            by += 1
+    return plan
+
+
+def collect_kernel(size, weights, slabs, plan, *refs):
+    shards = refs[:weights]
+    edges = refs[weights : weights + slabs]
+    refs = refs[weights + slabs :]
+    whole = refs[:weights]
+    halos = refs[weights : weights + 2 * len(plan)]
+    send, recv, own, edge_send, edge_recv = refs[weights + 2 * len(plan) :]
+    row = lax.axis_index("rows")
+    place = ring_place(row, size)
+    ahead = ring_row((place + 1) % size, size)
+    back = ring_row((place + size - 1) % size, size)
+    far = max(by for _, by, _ in plan)
+
+    barrier = pltpu.get_barrier_semaphore()
+    pl.semaphore_signal(barrier, inc=1, device_id={"rows": ahead}, device_id_type=MESH)
+    pl.semaphore_signal(barrier, inc=1, device_id={"rows": back}, device_id_type=MESH)
+    for by in range(1, far + 1):
+
+        @pl.when(row + by < size)
+        def _():
+            pl.semaphore_signal(barrier, inc=1, device_id={"rows": row + by}, device_id_type=MESH)
+
+        @pl.when(row >= by)
+        def _():
+            pl.semaphore_signal(barrier, inc=1, device_id={"rows": row - by}, device_id_type=MESH)
+
+    peers = 2 + jnp.minimum(row, far) + jnp.minimum(size - 1 - row, far)
+    pl.semaphore_wait(barrier, peers)
+
+    def hop(k, way, step):
+        origin = (place + size - step) % size if way == 0 else (place + step) % size
+        origin = ring_row(origin, size)
+        return pltpu.make_async_remote_copy(
+            src_ref=shards[k] if step == 0 else whole[k].at[origin],
+            dst_ref=whole[k].at[origin],
+            send_sem=send.at[k, way, step],
+            recv_sem=recv.at[k, way, step],
+            device_id={"rows": ahead if way == 0 else back},
+            device_id_type=MESH,
+        )
+
+    def edge(n, way):
+        k, by, take = plan[n]
+        rows = edges[k].shape[2]
+        first = rows - take if way == 0 else 0
+        other = row + by if way == 0 else row - by
+        return pltpu.make_async_remote_copy(
+            src_ref=edges[k].at[:, :, first : first + take],
+            dst_ref=halos[2 * n + way],
+            send_sem=edge_send.at[n, way],
+            recv_sem=edge_recv.at[n, way],
+            device_id={"rows": jnp.clip(other, 0, size - 1)},
+            device_id_type=MESH,
+        )
+
+    steps = (size // 2, size - 1 - size // 2)
+    local = []
+    for k in range(weights):
+        for way in range(2):
+            if steps[way] > 0:
+                hop(k, way, 0).start()
+        copy = pltpu.make_async_copy(shards[k], whole[k].at[row], own.at[k])
+        copy.start()
+        local.append(copy)
+    for n, (_, by, _) in enumerate(plan):
+
+        @pl.when(row + by < size)
+        def _():
+            edge(n, 0).start()
+
+        @pl.when(row >= by)
+        def _():
+            edge(n, 1).start()
+
+    for step in range(steps[0]):
+        for k in range(weights):
+            for way in range(2):
+                if step < steps[way]:
+                    hop(k, way, step).wait_recv()
+                    if step + 1 < steps[way]:
+                        hop(k, way, step + 1).start()
+    for k in range(weights):
+        local[k].wait()
+        for way in range(2):
+            for step in range(steps[way]):
+                hop(k, way, step).wait_send()
+    for n, (_, by, _) in enumerate(plan):
+
+        @pl.when(row + by < size)
+        def _():
+            edge(n, 0).wait_send()
+            edge(n, 1).wait_recv()
+
+        @pl.when(row >= by)
+        def _():
+            edge(n, 1).wait_send()
+            edge(n, 0).wait_recv()
+
+
+def collect(weights, slabs, widths):
     size = lax.axis_size("rows")
-    return lax.ppermute(array, "rows", [(i, i + by) for i in range(size - by)])
-
-
-def from_after(array, by=1):
-    size = lax.axis_size("rows")
-    return lax.ppermute(array, "rows", [(i + by, i) for i in range(size - by)])
+    plan = halo_plan([slab.shape for slab in slabs], widths)
+    out = [jax.ShapeDtypeStruct((size,) + w.shape, w.dtype) for w in weights]
+    for k, _, take in plan:
+        shape = slabs[k].shape
+        out += [jax.ShapeDtypeStruct(shape[:2] + (take,) + shape[3:], BF)] * 2
+    count = len(weights)
+    anywhere = pl.BlockSpec(memory_space=pl.ANY)
+    got = pl.pallas_call(
+        functools.partial(collect_kernel, size, count, len(slabs), plan),
+        in_specs=[anywhere] * (count + len(slabs)),
+        out_specs=[anywhere] * len(out),
+        out_shape=out,
+        scratch_shapes=[
+            pltpu.SemaphoreType.DMA((count, 2, size // 2 + 1)),
+            pltpu.SemaphoreType.DMA((count, 2, size // 2 + 1)),
+            pltpu.SemaphoreType.DMA((count,)),
+            pltpu.SemaphoreType.DMA((len(plan), 2)),
+            pltpu.SemaphoreType.DMA((len(plan), 2)),
+        ],
+        compiler_params=pltpu.CompilerParams(collective_id=0, has_side_effects=True),
+        name="collect",
+    )(*weights, *slabs)
+    full = [w.reshape((-1,) + w.shape[2:]) for w in got[:count]]
+    row = lax.axis_index("rows")
+    wide = []
+    for k, slab in enumerate(slabs):
+        before, after = [], []
+        for n, (at, by, _) in enumerate(plan):
+            if at == k:
+                zero = jnp.zeros((), BF)
+                before.insert(0, jnp.where(row >= by, got[count + 2 * n], zero))
+                after.append(jnp.where(row + by < size, got[count + 2 * n + 1], zero))
+        wide.append(jnp.concatenate(before + [slab] + after, axis=2))
+    return full, wide
+
+
+def across_kernel(size, mine_ref, out_ref, send, recv, own):
+    me = lax.axis_index("segment")
+    twin = me + 1 - 2 * (me % 2)
+    chips = size // 2
+    others = [(me + 2 * k) % size for k in range(1, chips)]
+    barrier = pltpu.get_barrier_semaphore()
+    for other in [twin] + others:
+        pl.semaphore_signal(barrier, inc=1, device_id={"segment": other}, device_id_type=MESH)
+    pl.semaphore_wait(barrier, chips)
+
+    def copy(n, source, slot, other):
+        return pltpu.make_async_remote_copy(
+            src_ref=source,
+            dst_ref=out_ref.at[slot],
+            send_sem=send.at[n],
+            recv_sem=recv.at[n],
+            device_id={"segment": other},
+            device_id_type=MESH,
+        )
+
+    far = [copy(k, mine_ref, me, other) for k, other in enumerate(others)]
+    for one in far:
+        one.start()
+    near = copy(chips - 1, mine_ref, me, twin)
+    near.start()
+    keep = pltpu.make_async_copy(mine_ref, out_ref.at[me], own.at[0])
+    keep.start()
+    passed = []
+    for k in range(1, chips):
+        far[k - 1].wait_recv()
+        origin = (me + size - 2 * k) % size
+        on = copy(chips - 1 + k, out_ref.at[origin], origin, twin)
+        on.start()
+        passed.append(on)
+    for one in far:
+        one.wait_send()
+    near.wait()
+    for on in passed:
+        on.wait()
+    keep.wait()
+
+
+def across(mine, number):
+    size = lax.axis_size("segment")
+    count = 2 * (size // 2) - 1
+    return pl.pallas_call(
+        functools.partial(across_kernel, size),
+        in_specs=[pl.BlockSpec(memory_space=pltpu.VMEM)],
+        out_specs=pl.BlockSpec(memory_space=pltpu.VMEM),
+        out_shape=jax.ShapeDtypeStruct((size,) + mine.shape, mine.dtype),
+        scratch_shapes=[
+            pltpu.SemaphoreType.DMA((count,)),
+            pltpu.SemaphoreType.DMA((count,)),
+            pltpu.SemaphoreType.DMA((1,)),
+        ],
+        compiler_params=pltpu.CompilerParams(collective_id=number, has_side_effects=True),
+        name="across",
+    )(mine)
 
 
 def stack_columns(window):
@@ -287,30 +499,24 @@
         width = array.shape[-1] // segments
         return lax.dynamic_slice_in_dim(array, segment * width, width, array.ndim - 1)
 
-    def gathered(weight):
-        return lax.all_gather(
-            weight.reshape(weight.shape[0], -1), "rows", axis=0, tiled=True
-        )
-
-    full = [
-        gathered(own_channels(weight_zero)),
-        gathered(own_channels(weight_one)),
-        gathered(own_channels(weight_two)),
-        gathered(weight_three),
-    ]
-
-    def with_rows(array, width):
-        rows = array.shape[2]
-        before = []
-        after = []
-        by = 1
-        while width > 0:
-            take = min(width, rows)
-            before.insert(0, from_before(array[:, :, rows - take :], by))
-            after.append(from_after(array[:, :, :take], by))
-            width -= take
-            by += 1
-        return jnp.concatenate(before + [array] + after, axis=2)
+    def flat(weight):
+        return weight.reshape(weight.shape[0], -1)
+
+    full, slabs = collect(
+        [
+            flat(own_channels(weight_zero)),
+            flat(own_channels(weight_one)),
+            flat(own_channels(weight_two)),
+            flat(weight_three),
+        ],
+        [features, cache_zero, cache_one, cache_two, cache_three.transpose(0, 1, 2, 4, 3)],
+        [2, 2, 2, 2, 1],
+    )
+    wide = slabs[0]
+    caches = slabs[1:]
+
+    def channels_joined(blocks):
+        return jnp.concatenate([blocks[k] for k in range(segments)], axis=-1)
 
     def inside(array, halo):
         rows = array.shape[2]
@@ -318,27 +524,19 @@
         keep = ((at >= halo) | (row > 0)) & ((at < rows - halo) | (row < row_devices - 1))
         return jnp.where(keep, array, jnp.zeros((), array.dtype))
 
-    wide = with_rows(features, 2)
-    caches = [
-        with_rows(cache_zero, 2),
-        with_rows(cache_one, 2),
-        with_rows(cache_two, 2),
-        with_rows(cache_three, 1),
-    ]
-
     width = weight_zero.shape[3] // segments
     window = jnp.concatenate([caches[0], activate(wide, gain_zero)], axis=1)
     total = convolve(window, full[0], width)
     total = total + own_channels(wide[:, :, 1:-1]).astype(F32)
     mine = inside(total.astype(BF), 1)
-    coarse = lax.all_gather(mine, "segment", axis=4, tiled=True)
+    coarse = channels_joined(across(mine, 1))
 
     width = weight_one.shape[3] // segments
     window = jnp.concatenate([caches[1], enlarge(activate(coarse, gain_one), 2)], axis=1)
     total = convolve(window, full[1], width)
     total = total + enlarge(mine, 2)[:, :, 1:-1].astype(F32)
     mine = inside(total.astype(BF), 1)
-    coarse = lax.all_gather(mine, "segment", axis=4, tiled=True)
+    coarse = channels_joined(across(mine, 2))
 
     width = weight_two.shape[3] // segments
     rows = caches[2].shape[2] - 2
@@ -353,7 +551,7 @@
         own_channels(proj_two),
         keep.astype(F32),
     )
-    coarse = lax.all_gather(mine, "segment", axis=1, tiled=True)
+    coarse = jnp.concatenate([blocks for blocks in across(mine, 3)], axis=1)
 
     own = frames // segments
     videos, channels = coarse.shape[:2]
@@ -367,7 +565,7 @@
         jnp.mean(widened * widened, axis=1, keepdims=True) + EPSILON
     )
     newest = jax.nn.silu(widened * gain_three[:, None]).astype(BF)
-    behind = caches[3].transpose(0, 1, 2, 4, 3)
+    behind = caches[3]
     behind = jnp.pad(behind, ((0, 0), (0, own), (0, 0), (0, 0), (0, 0)))
     swapped = jnp.concatenate([behind[:, 1:2], behind[:, 2:3], behind[:, 2:3]], axis=1)
     behind = jnp.where(segment * own == 0, behind, swapped)

time: 304 us -> 226 us (0.74)
  Pallas kernels: 36.5 us -> 168 us
  blocking collectives: 119 us -> 0 us
  starting transfers between devices: 41.1 us -> 0 us
  waiting for transfers between devices: 28.3 us -> 0 us
  between operations: 13.7 us -> 0.58 us
  local copies, waits for them, and re-layouts: 32.6 us -> 23.6 us
  other arithmetic: 17.9 us -> 22.1 us
    pallas_call x0 -> x4, Pallas kernels: none -> 131 us  [the longest x1 99.5 us: collect(): pl.pallas_call(functools.partial(collect_kernel, size, count, len(slabs),...]
    all_gather x4 -> x0, blocking collectives: 119 us -> none  [the longest x2 80.1 us: gathered(): lax.all_gather(weight.reshape(weight.shape[0], -1), 'rows', axis=0, tiled...]
    ppermute x14 -> x0, starting transfers between devices: 41 us -> none  [the longest x7 31.8 us: from_before(): return lax.ppermute(array, 'rows', [(i, i + by) for i in range(size - by)])]
    ppermute x14 -> x0, waiting for transfers between devices: 28.2 us -> none  [the longest x7 17.6 us: from_before(): return lax.ppermute(array, 'rows', [(i, i + by) for i in range(size - by)])]
    all_gather x3 -> x0, local copies, waits for them, and re-layouts: 9.49 us -> none  [the longest x2 8.07 us: shards(): coarse = lax.all_gather(mine, 'segment', axis=4, tiled=True)]
    another operation x0 -> x2, local copies, waits for them, and re-layouts: none -> 3.46 us  [the longest x1 2.14 us: shards(): taps = full[3].reshape(full[3].shape[0], 9, -1).transpose(1, 2, 0)]
    pallas_call x0 -> x1, local copies, waits for them, and re-layouts: none -> 3.2 us  [collect(): pl.pallas_call(functools.partial(collect_kernel, size, count, len(slabs),...]
    select_n x2, other arithmetic: 1.3 us -> 4.39 us  [inside(): return jnp.where(keep, array, jnp.zeros((), array.dtype))]
  transfers between devices with their start and end apart: 17 -> 0, of which waited for: 4 -> 0; matrix products, arithmetic and copies ran while one was open for 13% -> 0% of each run, Pallas kernels for 0% -> 0%
where the time goes in v2:
time: 226 us; the launch traced here: 225 us
  Pallas kernels  168 us (74%)
  local copies, waits for them, and re-layouts  23.6 us (10%)
  other arithmetic  22.1 us (10%)
  matrix products  10.6 us (5%)
    pallas_call x1, Pallas kernels, collect(): pl.pallas_call(functools.partial(collect_kernel, size, count, len(slabs),...  99.5 us
    pallas_call x3, Pallas kernels, across(): pl.pallas_call(functools.partial(across_kernel, size), in_specs=[pl.Block...  31.9 us
    pallas_call x1, Pallas kernels, middle(): pl.pallas_call(middle_kernel, grid=(videos,), in_specs=[one(cache.shape),...  25.3 us
    pallas_call x1, Pallas kernels, last(): pl.pallas_call(last_kernel, grid_spec=pltpu.PrefetchScalarGridSpec(num_sc...  11.4 us
    dot_general x2, matrix products, convolve(): product = jnp.dot(stacked, weight, preferred_element_type=F32)  10.6 us

profile of v2, /device:TPU:0, one launch (start us, length us, event | category | flops | bytes accessed | tf_op | source)
XLA Modules:
  0.0 225.0 jit_solution(6851315933859683755)
XLA Ops:
  0.0 1.6 constant_dynamic-slice_fusion.2
  1.8 1.0 reshape.189.refs_0_
  3.0 1.0 reshape.190.refs_1_
  5.3 0.8 reshape.192.refs_3_
  6.1 99.5 %collect.1 = (bf16[8,144,864]{2,1,0:T(8,128)(2,1)}, bf16[8,144,864]{2,1,0:T(8,128)(2,1)}, bf16[8,144,432]{2,1,0:T(8,128)(2,1)}, bf16[8,72,864]{2,1,0:T(8,128)(2,...) custom-call(bf16[144,864]{1,0:T(8,128)(2,1)} %reshape.189.refs_0_, ...), custom_call_target="tpu_custom_call" | custom-call | tf_op jit(solution)/shard_map/collect/pallas_call | solution.py:156
  105.7 0.8 select_dynamic-update-slice_fusion.3
  106.6 0.8 select_dynamic-update-slice_fusion.2
  107.5 0.9 constant_dynamic-update-slice_fusion.1
  108.5 0.9 select_dynamic-update-slice_fusion
  111.5 4.3 %fusion.16 = f32[2,6,5,16,864]{4,3,2,1,0:T(8,128)} fusion(bf16[1152,864,1,1,1]{1,0,4,3,2:T(8,128)(2,1)S(1)} %bitcast.52, bf16[2,6,5,16,384]{4,3,2,1,0:T(8,128)(2,1)S(1)} %get-tuple-element.56, bf16[2,4,5,16,384]{4,3,2,1,0:T(8,128)(2,1)S(1)} %fusion.55, bf16[2,2,5,16,384]{4,3,2,1,0:T(8,128)(2,1)S(1)} %select_dynamic-update-slice_fusion.2, ...), kind=kOutput, calls=%fused_computation.23 | convolution fusion | flops 1919877120 | bytes 7520256 | tf_op jit(solution)/shard_map/dot_general | solution.py:256
  115.9 2.8 %broadcast_select_fusion.7.mine_ref = bf16[2,4,3,16,96]{4,3,2,1,0:T(8,128)(2,1)} fusion(pred[3]{0:T(512)(128)(4,1)S(1)} %or_and_fusion, s32[]{:T(128)S(6)} %select_n.139, bf16[2,4,1,16,384]{4,3,2,1,0:T(8,128)(2,1)S(1)} %get-tuple-element.46, bf16[2,4,1,16,384]{4,3,2,1,0:T(8,128)(2,1)S(1)} %copy-done.4, ...), kind=kLoop, calls=%fused_computation.150 | loop fusion | flops 626688 | bytes 1695751 | tf_op jit(solution)/shard_map/jit(_where)/select_n | solution.py:525
  118.7 7.6 %across.3 = bf16[4,2,4,3,16,96]{5,4,3,2,1,0:T(8,128)(2,1)} custom-call(bf16[2,4,3,16,96]{4,3,2,1,0:T(8,128)(2,1)} %broadcast_select_fusion.7.mine_ref), custom_call_target="tpu_custom_call" | custom-call | tf_op jit(solution)/shard_map/across/pallas_call | solution.py:230
  126.3 1.1 slice_bitcast_fusion.11
  128.2 0.8 broadcast_in_dim.82
  129.5 1.0 broadcast_select_fusion.3
  130.5 1.0 select_maximum_fusion
  131.6 1.1 fusion.85
  133.1 6.3 %fusion = f32[2,6,6,32,864]{4,3,2,1,0:T(8,128)S(1)} fusion(bf16[1152,864,1,1,1]{1,0,4,3,2:T(8,128)(2,1)S(1)} %bitcast.51, bf16[2,6,6,32,384]{4,3,2,1,0:T(8,128)(2,1)S(1)} %get-tuple-element.50, bf16[2,4,6,32,384]{4,3,2,1,0:T(8,128)(2,1)S(1)} %reshape.195, bf16[2,2,2,32,384]{4,3,2,1,0:T(8,128)(2,1)S(1)} %broadcast_select_fusion.3, ...), kind=kOutput, calls=%fused_computation.2 | convolution fusion | flops 4618321920 | bytes 15261696 | tf_op jit(solution)/shard_map/dot_general | solution.py:256
  139.8 1.6 broadcast_select_fusion.2.mine_ref
  141.4 11.7 %across.4 = bf16[4,2,4,4,32,96]{5,4,3,2,1,0:T(8,128)(2,1)} custom-call(bf16[2,4,4,32,96]{4,3,2,1,0:T(8,128)(2,1)} %broadcast_select_fusion.2.mine_ref), custom_call_target="tpu_custom_call" | custom-call | tf_op jit(solution)/shard_map/across/pallas_call | solution.py:230
  153.1 1.3 slice_bitcast_fusion.7
  155.2 1.4 fusion.46.low_ref
  156.7 1.4 pad_maximum_fusion.1.cache_ref
  160.3 25.3 %middle.1.mine_ref = bf16[2,48,1536]{2,1,0:T(8,128)(2,1)} custom-call(bf16[2,2,8,64,384]{4,3,2,1,0:T(8,128)(2,1)} %pad_maximum_fusion.1.cache_ref, bf16[2,4,4,32,384]{4,3,2,1,0:T(8,128)(2,1)} %fusion.46.low_ref, bf16[2,4,4,32,384]{4,3,2,1,0:T(8,128)(2,1)} %copy-done.1, bf16[1152,432]{1,0:T(8,128)(2,1)} %bitcast.46, bf16[384,48]{1,0:T(8,128)(2,1)} %copy.49.proj_ref, ...), custom_call_target="tpu_custom_call" | custom-call | tf_op jit(solution)/shard_map/middle/pallas_call | solution.py:351
  185.6 12.6 %across.5 = bf16[4,2,48,1536]{3,2,1,0:T(8,128)(2,1)} custom-call(bf16[2,48,1536]{2,1,0:T(8,128)(2,1)} %middle.1.mine_ref), custom_call_target="tpu_custom_call" | custom-call | tf_op jit(solution)/shard_map/across/pallas_call | solution.py:230
  198.2 1.3 slice_bitcast_fusion.3
  200.3 1.6 fusion.32.low_ref
  202.9 1.0 slice.142
  204.1 2.8 %maximum_select_fusion.cache_ref = bf16[2,3,10,192,128]{4,3,2,1,0:T(8,128)(2,1)} fusion(bf16[2,1,10,192,128]{4,3,2,1,0:T(8,128)(2,1)S(1)} %slice.109, bf16[2,1,10,192,128]{4,3,2,1,0:T(8,128)(2,1)} %slice.142, bf16[2,2,10,192,128]{4,3,2,1,0:T(8,128)(2,1)S(1)} %pad_maximum_fusion, pred[]{:T(512)S(6)} %eq.3), kind=kLoop, calls=%fused_computation.17 | loop fusion | flops 4423680 | bytes 6881281 | tf_op jit(solution)/shard_map/jit(_where)/select_n | solution.py:571
  207.0 3.2 %copy.43 = bf16[8,72,864]{1,0,2:T(8,128)(2,1)S(1)} copy(bf16[8,72,864]{2,1,0:T(8,128)(2,1)} %get-tuple-element.40) | data formatting | bytes 1990656 | tf_op jit(solution)/shard_map/collect/pallas_call | solution.py:156
  210.2 2.1 reshape_reshape.3
  213.7 11.4 %last.1 = bf16[2,1,96,8,128]{4,3,2,1,0:T(8,128)(2,1)} custom-call(s32[3]{0:T(128)} %compare_convert_fusion.old_ref, bf16[2,3,10,192,128]{4,3,2,1,0:T(8,128)(2,1)} %maximum_select_fusion.cache_ref, bf16[2,192,1152]{2,1,0:T(8,128)(2,1)} %fusion.32.low_ref, bf16[2,192,384]{2,1,0:T(8,128)(2,1)} %slice.166.straight_ref, bf16[9,96,576]{2,1,0:T(8,128)(2,1)} %bitcast.44, ...), custom_call_target="tpu_custom_call" | custom-call | tf_op jit(solution)/shard_map/last/pallas_call | solution.py:450
  (85 shorter events, 12.2 us)
Async XLA Ops:
  0.0 4.0 %copy-start = (bf16[144,3,3,192]{3,0,2,1:T(8,128)(2,1)S(1)}, bf16[144,3,3,192]{3,0,2,1:T(8,128)(2,1)}, u32[]{:S(2)}) copy-start(bf16[144,3,3,192]{3,0,2,1:T(8,128)(2,1)} %param.26) | copy-start | bytes 1492996
  1.8 3.4 %copy-start.13 = (bf16[72,3,3,96]{3,0,2,1:T(8,128)(2,1)S(1)}, bf16[72,3,3,96]{3,0,2,1:T(8,128)(2,1)}, u32[]{:S(2)}) copy-start(bf16[72,3,3,96]{3,0,2,1:T(8,128)(2,1)} %param.27) | copy-start | bytes 373252
  5.3 100.5 %copy-start.12 = (bf16[2,2,1,16,384]{4,3,2,1,0:T(8,128)(2,1)S(1)}, bf16[2,2,1,16,384]{4,3,2,1,0:T(8,128)(2,1)}, u32[]{:S(2)}) copy-start(bf16[2,2,1,16,384]{4,3,2,1,0:T(8,128)(2,1)} %refs_5_.1) | copy-start | bytes 147460
  6.1 101.4 %copy-start.4 = (bf16[2,4,1,16,384]{4,3,2,1,0:T(8,128)(2,1)S(1)}, bf16[2,4,1,16,384]{4,3,2,1,0:T(8,128)(2,1)}, u32[]{:S(2)}) copy-start(bf16[2,4,1,16,384]{4,3,2,1,0:T(8,128)(2,1)} %refs_4_.1) | copy-start | bytes 294916
  105.6 4.0 %copy-start.15 = (f32[384]{0:T(512)S(1)}, f32[384]{0:T(512)}, u32[]{:S(2)}) copy-start(f32[384]{0:T(512)} %param.20) | copy-start | bytes 4612
  110.0 1.6 copy-start.20
  115.9 11.9 %copy-start.16 = (f32[384]{0:T(512)S(1)}, f32[384]{0:T(512)}, u32[]{:S(2)}) copy-start(f32[384]{0:T(512)} %param.21) | copy-start | bytes 4612
  128.2 2.3 %copy-start.11 = (bf16[2,2,2,32,384]{4,3,2,1,0:T(8,128)(2,1)S(1)}, bf16[2,2,2,32,384]{4,3,2,1,0:T(8,128)(2,1)}, u32[]{:S(2)}) copy-start(bf16[2,2,2,32,384]{4,3,2,1,0:T(8,128)(2,1)} %get-tuple-element.27) | copy-start | bytes 589828
  129.0 1.5 copy-start.6
  131.6 1.6 copy-start.19
  133.1 6.3 %copy-start.5 = (bf16[2,4,3,16,96]{4,3,2,1,0:T(8,128)(2,1)S(1)}, bf16[2,4,3,16,96]{4,3,2,1,0:T(8,128)(2,1)}, u32[]{:S(2)}) copy-start(bf16[2,4,3,16,96]{4,3,2,1,0:T(8,128)(2,1)} %broadcast_select_fusion.7.mine_ref) | copy-start | bytes 221188
  153.1 2.1 copy-start.17
  154.4 2.2 copy-start.8
  154.4 2.2 copy-start.7
  155.1 3.0 %copy-start.1 = (bf16[2,4,4,32,384]{4,3,2,1,0:T(8,128)(2,1)}, bf16[2,4,4,32,384]{4,3,2,1,0:T(8,128)(2,1)S(1)}, u32[]{:S(2)}) copy-start(bf16[2,4,4,32,384]{4,3,2,1,0:T(8,128)(2,1)S(1)} %get-tuple-element.44.straight_ref) | copy-start | bytes 2359300
  155.1 1.6 copy-start.3
  198.2 2.1 copy-start.18
  199.6 3.0 %copy-start.10 = (bf16[2,2,1,192,128]{4,3,2,1,0:T(8,128)(2,1)S(1)}, bf16[2,2,1,192,128]{4,3,2,1,0:T(8,128)(2,1)}, u32[]{:S(2)}) copy-start(bf16[2,2,1,192,128]{4,3,2,1,0:T(8,128)(2,1)} %get-tuple-element.24) | copy-start | bytes 589828
  199.6 3.0 %copy-start.9 = (bf16[2,2,1,192,128]{4,3,2,1,0:T(8,128)(2,1)S(1)}, bf16[2,2,1,192,128]{4,3,2,1,0:T(8,128)(2,1)}, u32[]{:S(2)}) copy-start(bf16[2,2,1,192,128]{4,3,2,1,0:T(8,128)(2,1)} %get-tuple-element.23) | copy-start | bytes 589828
  200.2 2.4 %copy-start.2 = (bf16[2,2,8,128,192]{3,4,2,1,0:T(8,128)(2,1)S(1)}, bf16[2,2,8,128,192]{3,4,2,1,0:T(8,128)(2,1)}, u32[]{:S(2)}) copy-start(bf16[2,2,8,128,192]{3,4,2,1,0:T(8,128)(2,1)} %param.19) | copy-start | bytes 4718596
  210.2 2.7 %copy-start.14 = (bf16[192,96]{1,0:T(8,128)(2,1)S(1)}, bf16[192,96]{1,0:T(8,128)(2,1)}, u32[]{:S(2)}) copy-start(bf16[192,96]{1,0:T(8,128)(2,1)} %param.29) | copy-start | bytes 110596

commit v3 on v2

--- a/solution.py
+++ b/solution.py
@@ -51,8 +51,10 @@
     refs = refs[weights + slabs :]
     whole = refs[:weights]
     halos = refs[weights : weights + 2 * len(plan)]
-    send, recv, own, edge_send, edge_recv = refs[weights + 2 * len(plan) :]
+    send, recv, own, edge_send, edge_recv, pass_send, pass_recv = refs[weights + 2 * len(plan) :]
     row = lax.axis_index("rows")
+    core = lax.axis_index("segment") % 2
+    twin = lax.axis_index("segment") + 1 - 2 * core
     place = ring_place(row, size)
     ahead = ring_row((place + 1) % size, size)
     back = ring_row((place + size - 1) % size, size)
@@ -61,6 +63,7 @@
     barrier = pltpu.get_barrier_semaphore()
     pl.semaphore_signal(barrier, inc=1, device_id={"rows": ahead}, device_id_type=MESH)
     pl.semaphore_signal(barrier, inc=1, device_id={"rows": back}, device_id_type=MESH)
+    pl.semaphore_signal(barrier, inc=1, device_id={"segment": twin}, device_id_type=MESH)
     for by in range(1, far + 1):
 
         @pl.when(row + by < size)
@@ -71,7 +74,7 @@
         def _():
             pl.semaphore_signal(barrier, inc=1, device_id={"rows": row - by}, device_id_type=MESH)
 
-    peers = 2 + jnp.minimum(row, far) + jnp.minimum(size - 1 - row, far)
+    peers = 3 + jnp.minimum(row, far) + jnp.minimum(size - 1 - row, far)
     pl.semaphore_wait(barrier, peers)
 
     def hop(k, way, step):
@@ -100,48 +103,75 @@
             device_id_type=MESH,
         )
 
-    steps = (size // 2, size - 1 - size // 2)
+    def pass_on(n, way):
+        return pltpu.make_async_remote_copy(
+            src_ref=halos[2 * n + way],
+            dst_ref=halos[2 * n + way],
+            send_sem=pass_send.at[n, way],
+            recv_sem=pass_recv.at[n, way],
+            device_id={"segment": twin},
+            device_id_type=MESH,
+        )
+
+    def steps(k, way):
+        return size // 2 - (way != min(k % 3, 1))
+
+    def each_edge(action):
+        for n, (_, by, _) in enumerate(plan):
+            above, below = row >= by, row + by < size
+            action(n, 0, below, above, core == n % 2)
+            action(n, 1, above, below, core == (n + 1) % 2)
+
+    def start(n, way, sends, receives, mine):
+        @pl.when(sends & mine)
+        def _():
+            edge(n, way).start()
+
+    def relay(n, way, sends, receives, mine):
+        @pl.when(receives & mine)
+        def _():
+            edge(n, way).wait_recv()
+            pass_on(n, way).start()
+
+    def finish(n, way, sends, receives, mine):
+        @pl.when(sends & mine)
+        def _():
+            edge(n, way).wait_send()
+
+        @pl.when(receives & mine)
+        def _():
+            pass_on(n, way).wait_send()
+
+        @pl.when(receives & jnp.logical_not(mine))
+        def _():
+            pass_on(n, way).wait_recv()
+
     local = []
     for k in range(weights):
         for way in range(2):
-            if steps[way] > 0:
+            if steps(k, way) > 0:
                 hop(k, way, 0).start()
         copy = pltpu.make_async_copy(shards[k], whole[k].at[row], own.at[k])
         copy.start()
         local.append(copy)
-    for n, (_, by, _) in enumerate(plan):
-
-        @pl.when(row + by < size)
-        def _():
-            edge(n, 0).start()
-
-        @pl.when(row >= by)
-        def _():
-            edge(n, 1).start()
-
-    for step in range(steps[0]):
+    each_edge(start)
+    for step in range(size // 2):
         for k in range(weights):
             for way in range(2):
-                if step < steps[way]:
+                if step < steps(k, way):
                     hop(k, way, step).wait_recv()
-                    if step + 1 < steps[way]:
+                    if step + 1 < steps(k, way):
                         hop(k, way, step + 1).start()
+        if step == size // 2 - 2:
+            each_edge(relay)
+    if size // 2 < 2:
+        each_edge(relay)
     for k in range(weights):
         local[k].wait()
         for way in range(2):
-            for step in range(steps[way]):
+            for step in range(steps(k, way)):
                 hop(k, way, step).wait_send()
-    for n, (_, by, _) in enumerate(plan):
-
-        @pl.when(row + by < size)
-        def _():
-            edge(n, 0).wait_send()
-            edge(n, 1).wait_recv()
-
-        @pl.when(row >= by)
-        def _():
-            edge(n, 1).wait_send()
-            edge(n, 0).wait_recv()
+    each_edge(finish)
 
 
 def collect(weights, slabs, widths):
@@ -164,6 +194,8 @@
             pltpu.SemaphoreType.DMA((count,)),
             pltpu.SemaphoreType.DMA((len(plan), 2)),
             pltpu.SemaphoreType.DMA((len(plan), 2)),
+            pltpu.SemaphoreType.DMA((len(plan), 2)),
+            pltpu.SemaphoreType.DMA((len(plan), 2)),
         ],
         compiler_params=pltpu.CompilerParams(collective_id=0, has_side_effects=True),
         name="collect",
@@ -285,27 +317,30 @@
     half = columns // 2
     line = rows * columns
     inner = rows - 2
-    for j in range(3):
-        fine = selector(columns, columns, j - 1, True)
-        coarse = selector(columns, half, j - 1, False)
-        lanes = slice(j * channels, (j + 1) * channels)
-
-        def old(w, _):
-            for q in range(rows):
-                at = pl.multiple_of(w * line + q * columns, columns)
-                stacked[pl.ds(at, columns), lanes] = picked(fine, cache_ref[0, w, q])
-            return 0
-
-        def new(f, _):
-            for l in range(rows // 2):
-                row = picked(coarse, low_ref[0, f, l])
-                at = pl.multiple_of((f + past) * line + 2 * l * columns, columns)
-                stacked[pl.ds(at, columns), lanes] = row
-                stacked[pl.ds(at + columns, columns), lanes] = row
-            return 0
-
-        lax.fori_loop(0, past, old, 0)
-        lax.fori_loop(0, frames, new, 0)
+    fine = jnp.concatenate([selector(columns, columns, j - 1, True) for j in range(3)], axis=0)
+    coarse = jnp.concatenate([selector(columns, half, j - 1, False) for j in range(3)], axis=0)
+
+    def put(at, row):
+        for j in range(3):
+            stacked[pl.ds(at, columns), j * channels : (j + 1) * channels] = row[
+                j * columns : (j + 1) * columns
+            ]
+
+    def old(w, _):
+        for q in range(rows):
+            put(pl.multiple_of(w * line + q * columns, columns), picked(fine, cache_ref[0, w, q]))
+        return 0
+
+    def new(f, _):
+        for l in range(rows // 2):
+            row = picked(coarse, low_ref[0, f, l])
+            at = pl.multiple_of((f + past) * line + 2 * l * columns, columns)
+            put(at, row)
+            put(at + columns, row)
+        return 0
+
+    lax.fori_loop(0, past, old, 0)
+    lax.fori_loop(0, frames, new, 0)
 
     coarse = selector(columns, half, 0, False)
 

time: 226 us -> 209 us (0.925)
  Pallas kernels: 168 us -> 149 us
    pallas_call x1, Pallas kernels: 99.5 us -> 84.3 us  [collect(): pl.pallas_call(functools.partial(collect_kernel, size, count, len(slabs),...]
    pallas_call x1, Pallas kernels: 25.3 us -> 21.9 us  [middle(): pl.pallas_call(middle_kernel, grid=(videos,), in_specs=[one(cache.shape),...]
where the time goes in v3:
time: 209 us; the launch traced here: 206 us
  Pallas kernels  149 us (71%)
  local copies, waits for them, and re-layouts  23.6 us (11%)
  other arithmetic  22.1 us (11%)
  matrix products  10.6 us (5%)
    pallas_call x1, Pallas kernels, collect(): pl.pallas_call(functools.partial(collect_kernel, size, count, len(slabs),...  84.3 us
    pallas_call x3, Pallas kernels, across(): pl.pallas_call(functools.partial(across_kernel, size), in_specs=[pl.Block...  31.6 us
    pallas_call x1, Pallas kernels, middle(): pl.pallas_call(middle_kernel, grid=(videos,), in_specs=[one(cache.shape),...  21.9 us
    pallas_call x1, Pallas kernels, last(): pl.pallas_call(last_kernel, grid_spec=pltpu.PrefetchScalarGridSpec(num_sc...  11.4 us
    dot_general x2, matrix products, convolve(): product = jnp.dot(stacked, weight, preferred_element_type=F32)  10.6 us
    select_n x2, other arithmetic, inside(): return jnp.where(keep, array, jnp.zeros((), array.dtype))  4.39 us

profile of v3, /device:TPU:0, one launch (start us, length us, event | category | flops | bytes accessed | tf_op | source)
XLA Modules:
  0.0 206.1 jit_solution(5400535524687529581)
XLA Ops:
  0.0 1.6 constant_dynamic-slice_fusion.2
  1.8 1.0 reshape.189.refs_0_
  3.0 1.0 reshape.190.refs_1_
  5.3 0.8 reshape.192.refs_3_
  6.1 84.3 %collect.1 = (bf16[8,144,864]{2,1,0:T(8,128)(2,1)}, bf16[8,144,864]{2,1,0:T(8,128)(2,1)}, bf16[8,144,432]{2,1,0:T(8,128)(2,1)}, bf16[8,72,864]{2,1,0:T(8,128)(2,...) custom-call(bf16[144,864]{1,0:T(8,128)(2,1)} %reshape.189.refs_0_, ...), custom_call_target="tpu_custom_call" | custom-call | tf_op jit(solution)/shard_map/collect/pallas_call | solution.py:186
  90.6 0.8 select_dynamic-update-slice_fusion.3
  91.4 0.8 select_dynamic-update-slice_fusion.2
  92.3 0.9 constant_dynamic-update-slice_fusion.1
  93.3 0.9 select_dynamic-update-slice_fusion
  96.4 4.3 %fusion.16 = f32[2,6,5,16,864]{4,3,2,1,0:T(8,128)} fusion(bf16[1152,864,1,1,1]{1,0,4,3,2:T(8,128)(2,1)S(1)} %bitcast.52, bf16[2,6,5,16,384]{4,3,2,1,0:T(8,128)(2,1)S(1)} %get-tuple-element.56, bf16[2,4,5,16,384]{4,3,2,1,0:T(8,128)(2,1)S(1)} %fusion.55, bf16[2,2,5,16,384]{4,3,2,1,0:T(8,128)(2,1)S(1)} %select_dynamic-update-slice_fusion.2, ...), kind=kOutput, calls=%fused_computation.23 | convolution fusion | flops 1919877120 | bytes 7520256 | tf_op jit(solution)/shard_map/dot_general | solution.py:288
  100.7 2.8 %broadcast_select_fusion.7.mine_ref = bf16[2,4,3,16,96]{4,3,2,1,0:T(8,128)(2,1)} fusion(pred[3]{0:T(512)(128)(4,1)S(1)} %or_and_fusion, s32[]{:T(128)S(6)} %select_n.139, bf16[2,4,1,16,384]{4,3,2,1,0:T(8,128)(2,1)S(1)} %get-tuple-element.46, bf16[2,4,1,16,384]{4,3,2,1,0:T(8,128)(2,1)S(1)} %copy-done.4, ...), kind=kLoop, calls=%fused_computation.150 | loop fusion | flops 626688 | bytes 1695751 | tf_op jit(solution)/shard_map/jit(_where)/select_n | solution.py:560
  103.5 7.4 %across.3 = bf16[4,2,4,3,16,96]{5,4,3,2,1,0:T(8,128)(2,1)} custom-call(bf16[2,4,3,16,96]{4,3,2,1,0:T(8,128)(2,1)} %broadcast_select_fusion.7.mine_ref), custom_call_target="tpu_custom_call" | custom-call | tf_op jit(solution)/shard_map/across/pallas_call | solution.py:262
  110.9 1.1 slice_bitcast_fusion.11
  112.8 0.8 broadcast_in_dim.82
  114.1 1.0 broadcast_select_fusion.3
  115.1 1.0 select_maximum_fusion
  116.2 1.1 fusion.85
  117.7 6.3 %fusion = f32[2,6,6,32,864]{4,3,2,1,0:T(8,128)S(1)} fusion(bf16[1152,864,1,1,1]{1,0,4,3,2:T(8,128)(2,1)S(1)} %bitcast.51, bf16[2,6,6,32,384]{4,3,2,1,0:T(8,128)(2,1)S(1)} %get-tuple-element.50, bf16[2,4,6,32,384]{4,3,2,1,0:T(8,128)(2,1)S(1)} %reshape.195, bf16[2,2,2,32,384]{4,3,2,1,0:T(8,128)(2,1)S(1)} %broadcast_select_fusion.3, ...), kind=kOutput, calls=%fused_computation.2 | convolution fusion | flops 4618321920 | bytes 15261696 | tf_op jit(solution)/shard_map/dot_general | solution.py:288
  124.4 1.6 broadcast_select_fusion.2.mine_ref
  126.0 11.7 %across.4 = bf16[4,2,4,4,32,96]{5,4,3,2,1,0:T(8,128)(2,1)} custom-call(bf16[2,4,4,32,96]{4,3,2,1,0:T(8,128)(2,1)} %broadcast_select_fusion.2.mine_ref), custom_call_target="tpu_custom_call" | custom-call | tf_op jit(solution)/shard_map/across/pallas_call | solution.py:262
  137.7 1.3 slice_bitcast_fusion.7
  139.8 1.4 fusion.46.low_ref
  141.3 1.4 pad_maximum_fusion.1.cache_ref
  144.9 21.9 %middle.1.mine_ref = bf16[2,48,1536]{2,1,0:T(8,128)(2,1)} custom-call(bf16[2,2,8,64,384]{4,3,2,1,0:T(8,128)(2,1)} %pad_maximum_fusion.1.cache_ref, bf16[2,4,4,32,384]{4,3,2,1,0:T(8,128)(2,1)} %fusion.46.low_ref, bf16[2,4,4,32,384]{4,3,2,1,0:T(8,128)(2,1)} %copy-done.1, bf16[1152,432]{1,0:T(8,128)(2,1)} %bitcast.46, bf16[384,48]{1,0:T(8,128)(2,1)} %copy.49.proj_ref, ...), custom_call_target="tpu_custom_call" | custom-call | tf_op jit(solution)/shard_map/middle/pallas_call | solution.py:386
  166.8 12.5 %across.5 = bf16[4,2,48,1536]{3,2,1,0:T(8,128)(2,1)} custom-call(bf16[2,48,1536]{2,1,0:T(8,128)(2,1)} %middle.1.mine_ref), custom_call_target="tpu_custom_call" | custom-call | tf_op jit(solution)/shard_map/across/pallas_call | solution.py:262
  179.3 1.3 slice_bitcast_fusion.3
  181.4 1.6 fusion.32.low_ref
  184.0 1.0 slice.142
  185.3 2.8 %maximum_select_fusion.cache_ref = bf16[2,3,10,192,128]{4,3,2,1,0:T(8,128)(2,1)} fusion(bf16[2,1,10,192,128]{4,3,2,1,0:T(8,128)(2,1)S(1)} %slice.109, bf16[2,1,10,192,128]{4,3,2,1,0:T(8,128)(2,1)} %slice.142, bf16[2,2,10,192,128]{4,3,2,1,0:T(8,128)(2,1)S(1)} %pad_maximum_fusion, pred[]{:T(512)S(6)} %eq.3), kind=kLoop, calls=%fused_computation.17 | loop fusion | flops 4423680 | bytes 6881281 | tf_op jit(solution)/shard_map/jit(_where)/select_n | solution.py:606
  188.1 3.2 %copy.43 = bf16[8,72,864]{1,0,2:T(8,128)(2,1)S(1)} copy(bf16[8,72,864]{2,1,0:T(8,128)(2,1)} %get-tuple-element.40) | data formatting | bytes 1990656 | tf_op jit(solution)/shard_map/collect/pallas_call | solution.py:186
  191.3 2.1 %reshape_reshape.3 = bf16[576,9,96]{0,2,1:T(8,128)(2,1)} reshape(bf16[8,72,864]{1,0,2:T(8,128)(2,1)S(1)} %copy.43) | data formatting | bytes 1990656 | tf_op jit(solution)/shard_map/reshape;reshape | solution.py:608
  194.8 11.4 %last.1 = bf16[2,1,96,8,128]{4,3,2,1,0:T(8,128)(2,1)} custom-call(s32[3]{0:T(128)} %compare_convert_fusion.old_ref, bf16[2,3,10,192,128]{4,3,2,1,0:T(8,128)(2,1)} %maximum_select_fusion.cache_ref, bf16[2,192,1152]{2,1,0:T(8,128)(2,1)} %fusion.32.low_ref, bf16[2,192,384]{2,1,0:T(8,128)(2,1)} %slice.166.straight_ref, bf16[9,96,576]{2,1,0:T(8,128)(2,1)} %bitcast.44, ...), custom_call_target="tpu_custom_call" | custom-call | tf_op jit(solution)/shard_map/last/pallas_call | solution.py:485
  (85 shorter events, 12.2 us)
Async XLA Ops:
  0.0 4.0 %copy-start = (bf16[144,3,3,192]{3,0,2,1:T(8,128)(2,1)S(1)}, bf16[144,3,3,192]{3,0,2,1:T(8,128)(2,1)}, u32[]{:S(2)}) copy-start(bf16[144,3,3,192]{3,0,2,1:T(8,128)(2,1)} %param.26) | copy-start | bytes 1492996
  1.8 3.4 %copy-start.13 = (bf16[72,3,3,96]{3,0,2,1:T(8,128)(2,1)S(1)}, bf16[72,3,3,96]{3,0,2,1:T(8,128)(2,1)}, u32[]{:S(2)}) copy-start(bf16[72,3,3,96]{3,0,2,1:T(8,128)(2,1)} %param.27) | copy-start | bytes 373252
  5.3 85.3 %copy-start.12 = (bf16[2,2,1,16,384]{4,3,2,1,0:T(8,128)(2,1)S(1)}, bf16[2,2,1,16,384]{4,3,2,1,0:T(8,128)(2,1)}, u32[]{:S(2)}) copy-start(bf16[2,2,1,16,384]{4,3,2,1,0:T(8,128)(2,1)} %refs_5_.1) | copy-start | bytes 147460
  6.1 86.2 %copy-start.4 = (bf16[2,4,1,16,384]{4,3,2,1,0:T(8,128)(2,1)S(1)}, bf16[2,4,1,16,384]{4,3,2,1,0:T(8,128)(2,1)}, u32[]{:S(2)}) copy-start(bf16[2,4,1,16,384]{4,3,2,1,0:T(8,128)(2,1)} %refs_4_.1) | copy-start | bytes 294916
  90.4 4.0 %copy-start.15 = (f32[384]{0:T(512)S(1)}, f32[384]{0:T(512)}, u32[]{:S(2)}) copy-start(f32[384]{0:T(512)} %param.20) | copy-start | bytes 4612
  94.8 1.6 copy-start.20
  100.7 11.6 %copy-start.16 = (f32[384]{0:T(512)S(1)}, f32[384]{0:T(512)}, u32[]{:S(2)}) copy-start(f32[384]{0:T(512)} %param.21) | copy-start | bytes 4612
  112.8 2.3 %copy-start.11 = (bf16[2,2,2,32,384]{4,3,2,1,0:T(8,128)(2,1)S(1)}, bf16[2,2,2,32,384]{4,3,2,1,0:T(8,128)(2,1)}, u32[]{:S(2)}) copy-start(bf16[2,2,2,32,384]{4,3,2,1,0:T(8,128)(2,1)} %get-tuple-element.27) | copy-start | bytes 589828
  113.6 1.5 copy-start.6
  116.2 1.6 copy-start.19
  117.7 6.3 %copy-start.5 = (bf16[2,4,3,16,96]{4,3,2,1,0:T(8,128)(2,1)S(1)}, bf16[2,4,3,16,96]{4,3,2,1,0:T(8,128)(2,1)}, u32[]{:S(2)}) copy-start(bf16[2,4,3,16,96]{4,3,2,1,0:T(8,128)(2,1)} %broadcast_select_fusion.7.mine_ref) | copy-start | bytes 221188
  137.7 2.1 %copy-start.17 = (f32[384]{0:T(512)S(1)}, f32[384]{0:T(512)}, u32[]{:S(2)}) copy-start(f32[384]{0:T(512)} %param.22) | copy-start | bytes 4612
  139.0 2.2 %copy-start.8 = (bf16[2,2,2,64,384]{4,3,2,1,0:T(8,128)(2,1)S(1)}, bf16[2,2,2,64,384]{4,3,2,1,0:T(8,128)(2,1)}, u32[]{:S(2)}) copy-start(bf16[2,2,2,64,384]{4,3,2,1,0:T(8,128)(2,1)} %get-tuple-element.26) | copy-start | bytes 1179652
  139.0 2.2 %copy-start.7 = (bf16[2,2,2,64,384]{4,3,2,1,0:T(8,128)(2,1)S(1)}, bf16[2,2,2,64,384]{4,3,2,1,0:T(8,128)(2,1)}, u32[]{:S(2)}) copy-start(bf16[2,2,2,64,384]{4,3,2,1,0:T(8,128)(2,1)} %get-tuple-element.25) | copy-start | bytes 1179652
  139.7 3.0 %copy-start.1 = (bf16[2,4,4,32,384]{4,3,2,1,0:T(8,128)(2,1)}, bf16[2,4,4,32,384]{4,3,2,1,0:T(8,128)(2,1)S(1)}, u32[]{:S(2)}) copy-start(bf16[2,4,4,32,384]{4,3,2,1,0:T(8,128)(2,1)S(1)} %get-tuple-element.44.straight_ref) | copy-start | bytes 2359300
  139.7 1.6 copy-start.3
  179.3 2.1 %copy-start.18 = (f32[192]{0:T(256)S(1)}, f32[192]{0:T(256)}, u32[]{:S(2)}) copy-start(f32[192]{0:T(256)} %param.23) | copy-start | bytes 2308
  180.7 3.0 %copy-start.10 = (bf16[2,2,1,192,128]{4,3,2,1,0:T(8,128)(2,1)S(1)}, bf16[2,2,1,192,128]{4,3,2,1,0:T(8,128)(2,1)}, u32[]{:S(2)}) copy-start(bf16[2,2,1,192,128]{4,3,2,1,0:T(8,128)(2,1)} %get-tuple-element.24) | copy-start | bytes 589828
  180.7 3.0 %copy-start.9 = (bf16[2,2,1,192,128]{4,3,2,1,0:T(8,128)(2,1)S(1)}, bf16[2,2,1,192,128]{4,3,2,1,0:T(8,128)(2,1)}, u32[]{:S(2)}) copy-start(bf16[2,2,1,192,128]{4,3,2,1,0:T(8,128)(2,1)} %get-tuple-element.23) | copy-start | bytes 589828
  181.4 2.4 %copy-start.2 = (bf16[2,2,8,128,192]{3,4,2,1,0:T(8,128)(2,1)S(1)}, bf16[2,2,8,128,192]{3,4,2,1,0:T(8,128)(2,1)}, u32[]{:S(2)}) copy-start(bf16[2,2,8,128,192]{3,4,2,1,0:T(8,128)(2,1)} %param.19) | copy-start | bytes 4718596
  191.3 2.7 %copy-start.14 = (bf16[192,96]{1,0:T(8,128)(2,1)S(1)}, bf16[192,96]{1,0:T(8,128)(2,1)}, u32[]{:S(2)}) copy-start(bf16[192,96]{1,0:T(8,128)(2,1)} %param.29) | copy-start | bytes 110596

commit v4 on v3

--- a/solution.py
+++ b/solution.py
@@ -428,14 +428,14 @@
     for t in range(3):
         flag = old_ref[t]
 
-        @pl.when(flag > 0)
+        @pl.when(flag >= 0)
         def _():
             for j in range(3):
                 fine = selector(columns, columns, j - 1, True, transposed=True)
                 for q in range(rows):
-                    put(t, j, q, picked(cache_ref[0, t, q], fine))
-
-        @pl.when(flag == 0)
+                    put(t, j, q, picked(cache_ref[0, jnp.maximum(flag, 0), q], fine))
+
+        @pl.when(flag < 0)
         def _():
             for j in range(3):
                 coarse = spread(j - 1)
@@ -600,13 +600,10 @@
         jnp.mean(widened * widened, axis=1, keepdims=True) + EPSILON
     )
     newest = jax.nn.silu(widened * gain_three[:, None]).astype(BF)
-    behind = caches[3]
-    behind = jnp.pad(behind, ((0, 0), (0, own), (0, 0), (0, 0), (0, 0)))
-    swapped = jnp.concatenate([behind[:, 1:2], behind[:, 2:3], behind[:, 2:3]], axis=1)
-    behind = jnp.where(segment * own == 0, behind, swapped)
-    old = (segment * own + jnp.arange(own + 2, dtype=jnp.int32) < 2).astype(jnp.int32)
+    at = segment * own + jnp.arange(own + 2, dtype=jnp.int32)
+    old = jnp.where(at < 2, at, -1)
     taps = full[3].reshape(full[3].shape[0], 9, -1).transpose(1, 2, 0)
-    return last(old, behind, newest, recent[:, :, 2 * cells :], taps, proj_three.T)
+    return last(old, caches[3], newest, recent[:, :, 2 * cells :], taps, proj_three.T)
 
 
 def solution(mesh):

time: 209 us -> 205 us (0.981)
    select_n x1, other arithmetic: 2.84 us -> 0.53 us  [shards(): old = jnp.where(at < 2, at, -1)]
where the time goes in v4:
time: 205 us; the launch traced here: 203 us
  Pallas kernels  149 us (73%)
  local copies, waits for them, and re-layouts  21.8 us (11%)
  other arithmetic  20.5 us (10%)
  matrix products  10.6 us (5%)
    pallas_call x1, Pallas kernels, collect(): pl.pallas_call(functools.partial(collect_kernel, size, count, len(slabs),...  84.3 us
    pallas_call x3, Pallas kernels, across(): pl.pallas_call(functools.partial(across_kernel, size), in_specs=[pl.Block...  31.6 us
    pallas_call x1, Pallas kernels, middle(): pl.pallas_call(middle_kernel, grid=(videos,), in_specs=[one(cache.shape),...  21.9 us
    pallas_call x1, Pallas kernels, last(): pl.pallas_call(last_kernel, grid_spec=pltpu.PrefetchScalarGridSpec(num_sc...  11.2 us
    dot_general x2, matrix products, convolve(): product = jnp.dot(stacked, weight, preferred_element_type=F32)  10.6 us
    concatenate x4, other arithmetic, collect(): wide.append(jnp.concatenate(before + [slab] + after, axis=2))  4.67 us
    select_n x2, other arithmetic, inside(): return jnp.where(keep, array, jnp.zeros((), array.dtype))  4.39 us

profile of v4, /device:TPU:0, one launch (start us, length us, event | category | flops | bytes accessed | tf_op | source)
XLA Modules:
  0.0 202.6 jit_solution(15899180833604028992)
XLA Ops:
  0.0 1.6 constant_dynamic-slice_fusion.2
  1.8 1.0 reshape.189.refs_0_
  3.0 1.0 reshape.190.refs_1_
  5.2 0.8 reshape.192.refs_3_
  6.1 84.3 %collect.1 = (bf16[8,144,864]{2,1,0:T(8,128)(2,1)}, bf16[8,144,864]{2,1,0:T(8,128)(2,1)}, bf16[8,144,432]{2,1,0:T(8,128)(2,1)}, bf16[8,72,864]{2,1,0:T(8,128)(2,...) custom-call(bf16[144,864]{1,0:T(8,128)(2,1)} %reshape.189.refs_0_, ...), custom_call_target="tpu_custom_call" | custom-call | tf_op jit(solution)/shard_map/collect/pallas_call | solution.py:186
  90.5 0.8 select_dynamic-update-slice_fusion.3
  91.4 0.8 select_dynamic-update-slice_fusion.2
  92.3 0.9 constant_dynamic-update-slice_fusion.1
  93.3 0.9 select_dynamic-update-slice_fusion
  95.7 1.2 copy-done.21
  96.9 4.3 %fusion.16 = f32[2,6,5,16,864]{4,3,2,1,0:T(8,128)} fusion(bf16[1152,864,1,1,1]{1,0,4,3,2:T(8,128)(2,1)S(1)} %bitcast.52, bf16[2,6,5,16,384]{4,3,2,1,0:T(8,128)(2,1)S(1)} %get-tuple-element.56, bf16[2,4,5,16,384]{4,3,2,1,0:T(8,128)(2,1)S(1)} %fusion.55, bf16[2,2,5,16,384]{4,3,2,1,0:T(8,128)(2,1)S(1)} %select_dynamic-update-slice_fusion.2, ...), kind=kOutput, calls=%fused_computation.22 | convolution fusion | flops 1919877120 | bytes 7520256 | tf_op jit(solution)/shard_map/dot_general | solution.py:288
  101.2 2.8 %broadcast_select_fusion.7.mine_ref = bf16[2,4,3,16,96]{4,3,2,1,0:T(8,128)(2,1)} fusion(pred[3]{0:T(512)(128)(4,1)S(1)} %or_and_fusion, s32[]{:T(128)S(6)} %select_n.135, bf16[2,4,1,16,384]{4,3,2,1,0:T(8,128)(2,1)S(1)} %get-tuple-element.46, bf16[2,4,1,16,384]{4,3,2,1,0:T(8,128)(2,1)S(1)} %copy-done.5, ...), kind=kLoop, calls=%fused_computation.149 | loop fusion | flops 626688 | bytes 1695751 | tf_op jit(solution)/shard_map/jit(_where)/select_n | solution.py:560
  104.0 7.4 %across.3 = bf16[4,2,4,3,16,96]{5,4,3,2,1,0:T(8,128)(2,1)} custom-call(bf16[2,4,3,16,96]{4,3,2,1,0:T(8,128)(2,1)} %broadcast_select_fusion.7.mine_ref), custom_call_target="tpu_custom_call" | custom-call | tf_op jit(solution)/shard_map/across/pallas_call | solution.py:262
  111.4 1.1 slice_bitcast_fusion.11
  113.3 0.8 broadcast_in_dim.87
  114.6 1.0 broadcast_select_fusion.3
  115.6 1.0 select_maximum_fusion
  116.7 1.1 fusion.85
  118.2 6.3 %fusion = f32[2,6,6,32,864]{4,3,2,1,0:T(8,128)S(1)} fusion(bf16[1152,864,1,1,1]{1,0,4,3,2:T(8,128)(2,1)S(1)} %bitcast.51, bf16[2,6,6,32,384]{4,3,2,1,0:T(8,128)(2,1)S(1)} %get-tuple-element.50, bf16[2,4,6,32,384]{4,3,2,1,0:T(8,128)(2,1)S(1)} %reshape.195, bf16[2,2,2,32,384]{4,3,2,1,0:T(8,128)(2,1)S(1)} %broadcast_select_fusion.3, ...), kind=kOutput, calls=%fused_computation.2 | convolution fusion | flops 4618321920 | bytes 15261696 | tf_op jit(solution)/shard_map/dot_general | solution.py:288
  124.9 1.6 broadcast_select_fusion.2.mine_ref
  126.5 11.7 %across.4 = bf16[4,2,4,4,32,96]{5,4,3,2,1,0:T(8,128)(2,1)} custom-call(bf16[2,4,4,32,96]{4,3,2,1,0:T(8,128)(2,1)} %broadcast_select_fusion.2.mine_ref), custom_call_target="tpu_custom_call" | custom-call | tf_op jit(solution)/shard_map/across/pallas_call | solution.py:262
  138.2 1.3 slice_bitcast_fusion.7
  140.3 1.4 fusion.46.low_ref
  141.8 1.4 pad_maximum_fusion.1.cache_ref
  145.4 21.9 %middle.1.mine_ref = bf16[2,48,1536]{2,1,0:T(8,128)(2,1)} custom-call(bf16[2,2,8,64,384]{4,3,2,1,0:T(8,128)(2,1)} %pad_maximum_fusion.1.cache_ref, bf16[2,4,4,32,384]{4,3,2,1,0:T(8,128)(2,1)} %fusion.46.low_ref, bf16[2,4,4,32,384]{4,3,2,1,0:T(8,128)(2,1)} %copy-done.1, bf16[1152,432]{1,0:T(8,128)(2,1)} %bitcast.46, bf16[384,48]{1,0:T(8,128)(2,1)} %copy.49.proj_ref, ...), custom_call_target="tpu_custom_call" | custom-call | tf_op jit(solution)/shard_map/middle/pallas_call | solution.py:386
  167.3 12.5 %across.5 = bf16[4,2,48,1536]{3,2,1,0:T(8,128)(2,1)} custom-call(bf16[2,48,1536]{2,1,0:T(8,128)(2,1)} %middle.1.mine_ref), custom_call_target="tpu_custom_call" | custom-call | tf_op jit(solution)/shard_map/across/pallas_call | solution.py:262
  179.9 1.3 slice_bitcast_fusion.3
  181.9 1.6 fusion.32.low_ref
  184.3 1.5 pad_maximum_fusion.cache_ref
  185.8 2.1 %copy.43 = bf16[8,72,864]{1,0,2:T(8,128)(2,1)S(1)} copy(bf16[8,72,864]{2,1,0:T(8,128)(2,1)S(1)} %copy-done.4) | data formatting | bytes 1990656 | tf_op jit(solution)/shard_map/collect/pallas_call | solution.py:186
  188.0 2.2 %reshape_reshape.3 = bf16[576,9,96]{0,2,1:T(8,128)(2,1)} reshape(bf16[8,72,864]{1,0,2:T(8,128)(2,1)S(1)} %copy.43) | data formatting | bytes 1990656 | tf_op jit(solution)/shard_map/reshape;reshape | solution.py:605
  191.4 11.2 %last.1 = bf16[2,1,96,8,128]{4,3,2,1,0:T(8,128)(2,1)} custom-call(s32[3]{0:T(128)} %compare_select_fusion.old_ref, bf16[2,2,10,192,128]{4,3,2,1,0:T(8,128)(2,1)} %pad_maximum_fusion.cache_ref, bf16[2,192,1152]{2,1,0:T(8,128)(2,1)} %fusion.32.low_ref, bf16[2,192,384]{2,1,0:T(8,128)(2,1)} %slice.155.straight_ref, bf16[9,96,576]{2,1,0:T(8,128)(2,1)} %bitcast.44, ...), custom_call_target="tpu_custom_call" | custom-call | tf_op jit(solution)/shard_map/last/pallas_call | solution.py:485
  (84 shorter events, 11.1 us)
Async XLA Ops:
  0.0 4.0 %copy-start = (bf16[144,3,3,192]{3,0,2,1:T(8,128)(2,1)S(1)}, bf16[144,3,3,192]{3,0,2,1:T(8,128)(2,1)}, u32[]{:S(2)}) copy-start(bf16[144,3,3,192]{3,0,2,1:T(8,128)(2,1)} %param.26) | copy-start | bytes 1492996
  1.8 3.3 %copy-start.14 = (bf16[72,3,3,96]{3,0,2,1:T(8,128)(2,1)S(1)}, bf16[72,3,3,96]{3,0,2,1:T(8,128)(2,1)}, u32[]{:S(2)}) copy-start(bf16[72,3,3,96]{3,0,2,1:T(8,128)(2,1)} %param.27) | copy-start | bytes 373252
  6.1 84.4 %copy-start.13 = (bf16[2,2,1,16,384]{4,3,2,1,0:T(8,128)(2,1)S(1)}, bf16[2,2,1,16,384]{4,3,2,1,0:T(8,128)(2,1)}, u32[]{:S(2)}) copy-start(bf16[2,2,1,16,384]{4,3,2,1,0:T(8,128)(2,1)} %refs_5_.1) | copy-start | bytes 147460
  6.1 86.2 %copy-start.5 = (bf16[2,4,1,16,384]{4,3,2,1,0:T(8,128)(2,1)S(1)}, bf16[2,4,1,16,384]{4,3,2,1,0:T(8,128)(2,1)}, u32[]{:S(2)}) copy-start(bf16[2,4,1,16,384]{4,3,2,1,0:T(8,128)(2,1)} %refs_4_.1) | copy-start | bytes 294916
  90.4 4.0 %copy-start.16 = (f32[384]{0:T(512)S(1)}, f32[384]{0:T(512)}, u32[]{:S(2)}) copy-start(f32[384]{0:T(512)} %param.20) | copy-start | bytes 4612
  95.3 1.6 copy-start.21
  101.2 11.6 %copy-start.17 = (f32[384]{0:T(512)S(1)}, f32[384]{0:T(512)}, u32[]{:S(2)}) copy-start(f32[384]{0:T(512)} %param.21) | copy-start | bytes 4612
  114.1 1.5 copy-start.12
  114.1 1.5 copy-start.7
  116.7 1.6 copy-start.20
  118.2 6.3 %copy-start.6 = (bf16[2,4,3,16,96]{4,3,2,1,0:T(8,128)(2,1)S(1)}, bf16[2,4,3,16,96]{4,3,2,1,0:T(8,128)(2,1)}, u32[]{:S(2)}) copy-start(bf16[2,4,3,16,96]{4,3,2,1,0:T(8,128)(2,1)} %broadcast_select_fusion.7.mine_ref) | copy-start | bytes 221188
  138.2 2.1 %copy-start.18 = (f32[384]{0:T(512)S(1)}, f32[384]{0:T(512)}, u32[]{:S(2)}) copy-start(f32[384]{0:T(512)} %param.22) | copy-start | bytes 4612
  139.5 2.2 %copy-start.9 = (bf16[2,2,2,64,384]{4,3,2,1,0:T(8,128)(2,1)S(1)}, bf16[2,2,2,64,384]{4,3,2,1,0:T(8,128)(2,1)}, u32[]{:S(2)}) copy-start(bf16[2,2,2,64,384]{4,3,2,1,0:T(8,128)(2,1)} %get-tuple-element.26) | copy-start | bytes 1179652
  139.5 2.2 %copy-start.8 = (bf16[2,2,2,64,384]{4,3,2,1,0:T(8,128)(2,1)S(1)}, bf16[2,2,2,64,384]{4,3,2,1,0:T(8,128)(2,1)}, u32[]{:S(2)}) copy-start(bf16[2,2,2,64,384]{4,3,2,1,0:T(8,128)(2,1)} %get-tuple-element.25) | copy-start | bytes 1179652
  140.2 3.0 %copy-start.1 = (bf16[2,4,4,32,384]{4,3,2,1,0:T(8,128)(2,1)}, bf16[2,4,4,32,384]{4,3,2,1,0:T(8,128)(2,1)S(1)}, u32[]{:S(2)}) copy-start(bf16[2,4,4,32,384]{4,3,2,1,0:T(8,128)(2,1)S(1)} %get-tuple-element.44.straight_ref) | copy-start | bytes 2359300
  140.2 1.6 copy-start.3
  179.8 2.1 %copy-start.19 = (f32[192]{0:T(256)S(1)}, f32[192]{0:T(256)}, u32[]{:S(2)}) copy-start(f32[192]{0:T(256)} %param.23) | copy-start | bytes 2308
  181.2 3.0 %copy-start.11 = (bf16[2,2,1,192,128]{4,3,2,1,0:T(8,128)(2,1)S(1)}, bf16[2,2,1,192,128]{4,3,2,1,0:T(8,128)(2,1)}, u32[]{:S(2)}) copy-start(bf16[2,2,1,192,128]{4,3,2,1,0:T(8,128)(2,1)} %get-tuple-element.24) | copy-start | bytes 589828
  181.9 2.4 %copy-start.10 = (bf16[2,2,1,192,128]{4,3,2,1,0:T(8,128)(2,1)S(1)}, bf16[2,2,1,192,128]{4,3,2,1,0:T(8,128)(2,1)}, u32[]{:S(2)}) copy-start(bf16[2,2,1,192,128]{4,3,2,1,0:T(8,128)(2,1)} %get-tuple-element.23) | copy-start | bytes 589828
  181.9 2.4 %copy-start.2 = (bf16[2,2,8,128,192]{3,4,2,1,0:T(8,128)(2,1)S(1)}, bf16[2,2,8,128,192]{3,4,2,1,0:T(8,128)(2,1)}, u32[]{:S(2)}) copy-start(bf16[2,2,8,128,192]{3,4,2,1,0:T(8,128)(2,1)} %param.19) | copy-start | bytes 4718596
  184.3 1.5 copy-start.4
  188.0 2.7 %copy-start.15 = (bf16[192,96]{1,0:T(8,128)(2,1)S(1)}, bf16[192,96]{1,0:T(8,128)(2,1)}, u32[]{:S(2)}) copy-start(bf16[192,96]{1,0:T(8,128)(2,1)} %param.29) | copy-start | bytes 110596
